TPU v7x, 256 devices: a whole 4x4x8 slice. The times are simulated.
256 devices in a mesh: mem: 16 (over x_hi, y, core), tile: 16 (over x_lo, z).
Axes of the slice: x: 4 (x_hi: 2, x_lo: 2; x = x_hi * 2 + x_lo), y: 4, z: 8, core: 2. Of those that a mesh axis runs over, the one named last changes fastest.
Arguments:
- alpha: bfloat16 [16, 16, 720, 1440], P('mem', None, 'tile'), may hold values from -6 to 6
- perturbation: bfloat16 [16, 16, 720, 1440], P('mem', None, 'tile'), may hold values from -3 to 3
- lon_scale: float32 [16], replicated, may hold values from 8 to 48
- lat_scale: float32 [16], replicated, may hold values from 12 to 64
- obs_level: int32 [16, 16384], P('tile'), may hold values from 0 to 15
- obs_row: int32 [16, 16384], P('tile'), may hold values from 0 to 44
- obs_col: int32 [16, 16384], P('tile'), may hold values from 0 to 1439
- obs_count: int32 [16], P('tile'), may hold values from 8192 to 16384, as said below
- innovation: float32 [16, 16384], P('tile'), may hold values from -12 to 12
- obs_weight: float32 [16, 16384], P('tile'), may hold values from 1 to 8
Outputs:
- gradient: bfloat16 [16, 16, 720, 1440], P('mem', None, 'tile')
Inputs may be any that keep to these rules, and one draw needn't show every extreme that they name: Observations of band t fill slots 0 to obs_count[t] - 1; the other slots carry no observation. Some band is full in every draw.
All inputs are finite; a program needn't handle non-finite values.
Results may differ from a plain program's by a relative error of at most 0.0056.
Values may be sent and summed in bfloat16 or wider, within the bound.
No kernel may reach another device: no remote copies, remote signals or barrier semaphores. Data moves between devices by JAX's collectives and lax.ppermute only.
A program may use at most 128 MiB of HBM per device.

v0:
```python
import jax
import jax.numpy as jnp
from jax import lax
from jax.sharding import PartitionSpec as P


def square_root(lengths, extent, periodic):
    positions = jnp.arange(extent).astype(jnp.float32)
    distance = jnp.abs(positions[:, None] - positions[None, :])
    if periodic:
        distance = jnp.minimum(distance, extent - distance)
    scales = lengths[:, None, None]
    factor = (2.0 / jnp.pi) ** 0.25
    values = factor * jnp.exp(-((distance[None] / scales) ** 2)) / jnp.sqrt(scales)
    return values.astype(jnp.bfloat16)


def localize(values_in, lat_root, lon_root):
    zonal = jnp.einsum(
        "klab,lbc->klac", values_in, lon_root, preferred_element_type=jnp.float32
    ).astype(jnp.bfloat16)
    return jnp.einsum("lab,klbc->klac", lat_root, zonal, preferred_element_type=jnp.float32)


def pick_cells(flat_rows, row_place, column):
    slots = row_place.shape[0]
    block = min(4096, slots)
    width = flat_rows.shape[1]
    counter = jnp.arange(width)

    def pick_one_block(pair):
        rows_here, cols_here = pair
        taken = flat_rows[rows_here]
        return jnp.sum(jnp.where(counter[None, :] == cols_here[:, None], taken, 0.0), axis=1)

    picked = lax.map(pick_one_block, (row_place.reshape(-1, block), column.reshape(-1, block)))
    return picked.reshape(-1)


def place_cells(row_total, width, row_place, column, values):
    slots = row_place.shape[0]
    block = min(4096, slots)
    counter = jnp.arange(width)

    def place_one_block(field, triple):
        rows_here, cols_here, vals_here = triple
        lines = jnp.where(counter[None, :] == cols_here[:, None], vals_here[:, None], 0.0)
        return (field.at[rows_here].add(lines, mode="drop"), jnp.float32(0.0))

    start_field = jnp.zeros((row_total, width), jnp.float32)
    triples = (row_place.reshape(-1, block), column.reshape(-1, block), values.reshape(-1, block))
    return lax.scan(place_one_block, start_field, triples)[0]


def shards(
    alpha,
    perturbation,
    lon_scale,
    lat_scale,
    obs_level,
    obs_row,
    obs_col,
    obs_count,
    innovation,
    obs_weight,
):
    level_count = alpha.shape[1]
    row_count = alpha.shape[2]
    column_count = alpha.shape[3]
    tile_count = lax.axis_size("tile")
    tile_index = lax.axis_index("tile")
    slab_levels = level_count // tile_count
    first_level = tile_index * slab_levels
    lon_part = lax.dynamic_slice_in_dim(lon_scale, first_level, slab_levels)
    lat_part = lax.dynamic_slice_in_dim(lat_scale, first_level, slab_levels)
    lon_root = square_root(lon_part, column_count, True)
    lat_root = square_root(lat_part, row_count * tile_count, False)
    level_index = obs_level[0]
    row_index = obs_row[0]
    column = obs_col[0]
    slot_count = obs_level.shape[1]
    valid = jnp.arange(slot_count) < obs_count[0]
    band_line = level_index * row_count + row_index
    alpha_slab = lax.all_to_all(alpha, "tile", split_axis=1, concat_axis=2, tiled=True)
    spread_slab = localize(alpha_slab, lat_root, lon_root).astype(jnp.bfloat16)
    spread_band = lax.all_to_all(spread_slab, "tile", split_axis=2, concat_axis=1, tiled=True)
    partial_field = jnp.sum(
        perturbation.astype(jnp.float32) * spread_band.astype(jnp.float32), axis=0
    )
    total_field = lax.psum(partial_field, "mem")
    model_obs = pick_cells(total_field.reshape(-1, column_count), band_line, column)
    weighted = jnp.where(valid, obs_weight[0] * (model_obs - innovation[0]), 0.0)
    obs_field = place_cells(level_count * row_count, column_count, band_line, column, weighted)
    obs_field = obs_field.reshape(level_count, row_count, column_count)
    sensitive = (perturbation.astype(jnp.float32) * obs_field[None]).astype(jnp.bfloat16)
    sensitive_slab = lax.all_to_all(sensitive, "tile", split_axis=1, concat_axis=2, tiled=True)
    gradient_slab = (
        alpha_slab.astype(jnp.float32) + localize(sensitive_slab, lat_root, lon_root)
    ).astype(jnp.bfloat16)
    return lax.all_to_all(gradient_slab, "tile", split_axis=2, concat_axis=1, tiled=True)


def solution(mesh):
    in_specs = (
        P("mem", None, "tile", None),
        P("mem", None, "tile", None),
        P(),
        P(),
        P("tile", None),
        P("tile", None),
        P("tile", None),
        P("tile"),
        P("tile", None),
        P("tile", None),
    )
    out_specs = P("mem", None, "tile", None)
    return jax.shard_map(shards, mesh=mesh, in_specs=in_specs, out_specs=out_specs, check_vma=False)
```

profile of v0, /device:TPU:32, one launch (start us, length us, event | category | flops | bytes accessed | tf_op | source)
XLA Modules:
  0.0 922.2 jit_solution(17614433650385890455)
XLA Ops:
  23.2 51.6 %all-to-all-done = bf16[1,16,45,1440]{3,2,0,1:T(8,128)(2,1)S(1)} async-done(((bf16[1,16,45,1440]{3,2,0,1:T(8,128)(2,1)}), bf16[1,16,45,1440]{3,2,0,1:T(8,128)(2,1)S(1)}, u32[]{:S(2)}, u32[]{:S(2)}) %all-to-all-start) | async-done | bytes 2073632 | tf_op jit(solution)/shard_map/all_to_all | solution.py:84
  77.0 11.9 %fusion.29 = bf16[1,1,720,1440]{2,3,0,1:T(8,128)(2,1)} fusion(bf16[720,1440]{1,0:T(8,128)(2,1)} %reshape.399, f32[]{:T(128)} %bitcast.1, f32[]{:T(128)} %bitcast, f32[1440]{0:T(1024)S(1)} %iota_convert_fusion, f32[]{:T(128)} %bitcast.8, f32[]{:T(128)} %bitcast.7, f32[720]{0:T(1024)S(1)} %iota_convert_fusion.1), kind=kOutput, calls=%fused_computation.37 | convolution fusion | flops 4505932800 | bytes 4155856 | tf_op jit(solution)/shard_map/lab,klbc->klac/dot_general | solution.py:22
  88.9 12.1 %copy.33 = bf16[1,1,720,1440]{3,0,1,2:T(2,128)(2,1)} copy(bf16[1,1,720,1440]{2,3,0,1:T(8,128)(2,1)} %fusion.29) | data formatting | bytes 4147200 | tf_op jit(solution)/shard_map/convert_element_type | solution.py:85
  101.5 13.8 %reduce.18 = bf16[720,1440]{1,0:T(8,128)(2,1)S(1)} reduce(bf16[720,1,1,1440]{3,2,1,0:T(2,128)(2,1)} %bitcast.101, bf16[]{:T(256)} %broadcast.349), dimensions={1,2}, to_apply=%bitcast.69.reduce_sub_computation | reduce | bytes 4147202
  120.9 55.2 %all_to_all.19 = bf16[16,2,32400]{2,1,0:T(2,128)(2,1)S(1)} all-to-all(bf16[16,2,32400]{2,1,0:T(2,128)(2,1)} %reshape.462), channel_id=1, replica_groups=mesh['mem'=16,'tile'=16] {'tile'}, dimensions={0} | all-to-all | bytes 4147200 | tf_op jit(solution)/shard_map/all_to_all | solution.py:86
  211.9 148.9 %all-reduce.2.cloned.1.call-done = f32[720,1440]{1,0:T(8,128)} async-done(((f32[720,1440]{1,0:T(8,128)}), f32[720,1440]{1,0:T(8,128)}) %all-reduce.2.cloned.1.call-update) | async-done | bytes 4147216 | tf_op jit(solution)/shard_map/psum | solution.py:90
  360.8 162.4 %while.24 = (s32[]{:T(128)}, f32[4,4096]{1,0:T(4,128)S(1)}, s32[4,4096]{1,0:T(4,128)S(1)}, s32[4,4096]{1,0:T(4,128)S(1)}, f32[720,1440]{1,0:T(8,128)}) while((s32[]{:T(128)}, f32[4,4096]{1,0:T(4,128)S(1)}, s32[4,4096]{1,0:T(4,128)S(1)}, s32[4,4096]{1,0:T(4,128)S(1)}, f32[720,1440]{1,0:T(8,128)}) %tuple.43), condition=%wide.region_3.4_spmd.clone.clone, body=%wide.region_1.3_spmd.clone.sunk.clone | while | flops 17707008 | bytes 70959168 | solution.py:36
  360.8 29.5 %gather_fusion = f32[4096,1440]{1,0:T(8,128)} fusion(f32[720,1440]{1,0:T(8,128)} %get-tuple-element.217, s32[4096]{0:T(1024)S(1)} %broadcast_clamp_fusion.3), kind=kCustom, calls=%fused_computation.clone.clone.1.clone | custom fusion | bytes 47202304 | tf_op jit(solution)/shard_map/while/body/eval_jaxpr/gather | solution.py:33
  401.4 29.4 %gather_fusion = f32[4096,1440]{1,0:T(8,128)} fusion(f32[720,1440]{1,0:T(8,128)} %get-tuple-element.217, s32[4096]{0:T(1024)S(1)} %broadcast_clamp_fusion.3), kind=kCustom, calls=%fused_computation.clone.clone.1.clone | custom fusion | bytes 47202304 | tf_op jit(solution)/shard_map/while/body/eval_jaxpr/gather | solution.py:33
  430.8 10.8 %select_reduce_fusion.3 = f32[4096]{0:T(1024)S(1)} fusion(f32[4096,1440]{1,0:T(8,128)} %gather_fusion, s32[4096]{0:T(1024)S(1)} %bitcast.107), kind=kLoop, calls=%fused_computation.5.clone.1.clone | loop fusion | flops 17690624 | bytes 23625728 | tf_op jit(solution)/shard_map/while/body/eval_jaxpr/reduce_sum | solution.py:34
  441.9 29.4 %gather_fusion = f32[4096,1440]{1,0:T(8,128)} fusion(f32[720,1440]{1,0:T(8,128)} %get-tuple-element.217, s32[4096]{0:T(1024)S(1)} %broadcast_clamp_fusion.3), kind=kCustom, calls=%fused_computation.clone.clone.1.clone | custom fusion | bytes 47202304 | tf_op jit(solution)/shard_map/while/body/eval_jaxpr/gather | solution.py:33
  482.5 29.4 %gather_fusion = f32[4096,1440]{1,0:T(8,128)} fusion(f32[720,1440]{1,0:T(8,128)} %get-tuple-element.217, s32[4096]{0:T(1024)S(1)} %broadcast_clamp_fusion.3), kind=kCustom, calls=%fused_computation.clone.clone.1.clone | custom fusion | bytes 47202304 | tf_op jit(solution)/shard_map/while/body/eval_jaxpr/gather | solution.py:33
  512.0 10.8 %select_reduce_fusion.3 = f32[4096]{0:T(1024)S(1)} fusion(f32[4096,1440]{1,0:T(8,128)} %gather_fusion, s32[4096]{0:T(1024)S(1)} %bitcast.107), kind=kLoop, calls=%fused_computation.5.clone.1.clone | loop fusion | flops 17690624 | bytes 23625728 | tf_op jit(solution)/shard_map/while/body/eval_jaxpr/reduce_sum | solution.py:34
  525.9 188.8 %while.25 = (s32[]{:T(128)}, f32[720,1440]{1,0:T(8,128)}, s32[4,4096]{1,0:T(4,128)S(1)}, s32[4,4096]{1,0:T(4,128)S(1)}, f32[4,4096]{1,0:T(4,128)S(1)}) while((s32[]{:T(128)}, f32[720,1440]{1,0:T(8,128)}, s32[4,4096]{1,0:T(4,128)S(1)}, s32[4,4096]{1,0:T(4,128)S(1)}, f32[4,4096]{1,0:T(4,128)S(1)}) %tuple.52), condition=%wide.region_6.7_spmd.clone.clone, body=%wide.region_4.6_spmd.clone.sunk.clone | while | flops 17707008 | bytes 4278857 | solution.py:52
  526.0 47.1 %scatter_custom_fusion.8 = f32[720,1440]{1,0:T(8,128)} fusion(f32[720,1440]{1,0:T(8,128)} %get-tuple-element.224, s32[4096]{0:T(1024)S(1)} %bitcast.109, f32[]{:T(128)} %constant.35.clone.1..sunk.1, f32[4096]{0:T(1024)S(1)} %bitcast.105, s32[4096]{0:T(1024)S(1)} %bitcast.106), kind=kCustom, calls=%fused_computation.10.clone.1.clone | custom fusion | flops 17694720 | bytes 4180480 | tf_op jit(solution)/shard_map/while/body/eval_jaxpr/scatter-add | solution.py:48
  573.2 47.1 %scatter_custom_fusion.8 = f32[720,1440]{1,0:T(8,128)} fusion(f32[720,1440]{1,0:T(8,128)} %get-tuple-element.224, s32[4096]{0:T(1024)S(1)} %bitcast.109, f32[]{:T(128)} %constant.35.clone.1..sunk.1, f32[4096]{0:T(1024)S(1)} %bitcast.105, s32[4096]{0:T(1024)S(1)} %bitcast.106), kind=kCustom, calls=%fused_computation.10.clone.1.clone | custom fusion | flops 17694720 | bytes 4180480 | tf_op jit(solution)/shard_map/while/body/eval_jaxpr/scatter-add | solution.py:48
  620.3 47.1 %scatter_custom_fusion.8 = f32[720,1440]{1,0:T(8,128)} fusion(f32[720,1440]{1,0:T(8,128)} %get-tuple-element.224, s32[4096]{0:T(1024)S(1)} %bitcast.109, f32[]{:T(128)} %constant.35.clone.1..sunk.1, f32[4096]{0:T(1024)S(1)} %bitcast.105, s32[4096]{0:T(1024)S(1)} %bitcast.106), kind=kCustom, calls=%fused_computation.10.clone.1.clone | custom fusion | flops 17694720 | bytes 4180480 | tf_op jit(solution)/shard_map/while/body/eval_jaxpr/scatter-add | solution.py:48
  667.5 47.1 %scatter_custom_fusion.8 = f32[720,1440]{1,0:T(8,128)} fusion(f32[720,1440]{1,0:T(8,128)} %get-tuple-element.224, s32[4096]{0:T(1024)S(1)} %bitcast.109, f32[]{:T(128)} %constant.35.clone.1..sunk.1, f32[4096]{0:T(1024)S(1)} %bitcast.105, s32[4096]{0:T(1024)S(1)} %bitcast.106), kind=kCustom, calls=%fused_computation.10.clone.1.clone | custom fusion | flops 17694720 | bytes 4180480 | tf_op jit(solution)/shard_map/while/body/eval_jaxpr/scatter-add | solution.py:48
  741.7 12.2 %copy.38 = f32[1,1,720,1440]{2,3,0,1:T(8,128)} copy(f32[1,1,720,1440]{3,0,2,1:T(1,128)} %reshape.405) | data formatting | bytes 8294400 | tf_op jit(solution)/shard_map/convert_element_type | solution.py:98
  753.9 33.5 %all-to-all-done.2 = bf16[1,16,45,1440]{3,2,0,1:T(8,128)(2,1)} async-done(((bf16[1,16,45,1440]{3,2,0,1:T(8,128)(2,1)}), bf16[1,16,45,1440]{3,2,0,1:T(8,128)(2,1)}, u32[]{:S(2)}, u32[]{:S(2)}) %all-to-all-start.2) | async-done | bytes 2073632 | tf_op jit(solution)/shard_map/all_to_all | solution.py:96
  790.8 11.8 %fusion.18 = bf16[1,1,720,1440]{2,3,0,1:T(8,128)(2,1)S(1)} fusion(f32[1,1,720,1440]{2,3,0,1:T(8,128)} %copy.38, bf16[720,1440]{1,0:T(8,128)(2,1)} %reshape.402, f32[]{:T(128)} %bitcast.1, f32[]{:T(128)} %bitcast, f32[1440]{0:T(1024)S(1)} %copy-done.12, f32[]{:T(128)} %bitcast.8, f32[]{:T(128)} %bitcast.7, f32[720]{0:T(1024)S(1)} %copy-done.14), kind=kOutput, calls=%fused_computation.31 | convolution fusion | flops 4506969600 | bytes 8303056 | tf_op jit(solution)/shard_map/lab,klbc->klac/dot_general | solution.py:22
  811.9 14.1 %reduce.19 = bf16[720,1440]{1,0:T(8,128)(2,1)S(1)} reduce(bf16[720,1,1,1440]{3,2,1,0:T(2,128)(2,1)} %bitcast.102, bf16[]{:T(256)} %broadcast.349), dimensions={1,2}, to_apply=%bitcast.71.reduce_sub_computation | reduce | bytes 4147202
  831.1 55.3 %all_to_all.40 = bf16[16,2,32400]{2,1,0:T(2,128)(2,1)S(1)} all-to-all(bf16[16,2,32400]{2,1,0:T(2,128)(2,1)} %reshape.464), channel_id=1, replica_groups=mesh['mem'=16,'tile'=16] {'tile'}, dimensions={0} | all-to-all | bytes 4147200 | tf_op jit(solution)/shard_map/all_to_all | solution.py:100
  895.0 15.3 %bitcast_reduce_fusion = bf16[720,1440]{1,0:T(8,128)(2,1)} fusion(bf16[720,1,1,1440]{3,2,1,0:T(2,128)(2,1)} %reshape.465), kind=kLoop, calls=%fused_computation.51 | loop fusion | bytes 4147200 | tf_op jit(solution)/shard_map/all_to_all | solution.py:100
  (104 shorter events, 142.3 us)
Async XLA Ops:
  6.5 13.8 %copy-start.15 = (f32[16]{0:T(128)S(1)}, f32[16]{0:T(128)}, u32[]{:S(2)}) copy-start(f32[16]{0:T(128)} %param.16) | copy-start | bytes 196
  6.5 15.2 %copy-start.16 = (f32[16]{0:T(128)S(1)}, f32[16]{0:T(128)}, u32[]{:S(2)}) copy-start(f32[16]{0:T(128)} %param.17) | copy-start | bytes 196
  10.8 64.0 %all-to-all-start = ((bf16[1,16,45,1440]{3,2,0,1:T(8,128)(2,1)}), bf16[1,16,45,1440]{3,2,0,1:T(8,128)(2,1)S(1)}, u32[]{:S(2)}, u32[]{:S(2)}) async-start(bf16[1,16,45,1440]{3,2,0,1:T(8,128)(2,1)} %copy.32), calls=%async_computation | async-start | bytes 4718592 | tf_op jit(solution)/shard_map/all_to_all | solution.py:84
  20.3 340.4 %all-reduce.2.cloned.1.call-start = ((), (), s32[]{:S(2)}) async-start(), calls=%async_computation.4 | async-start | bytes 8847360 | tf_op jit(solution)/shard_map/psum | solution.py:90
  23.2 65.7 %copy-start.13 = (f32[720]{0:T(1024)}, f32[720]{0:T(1024)S(1)}, u32[]{:S(2)}) copy-start(f32[720]{0:T(1024)S(1)} %iota_convert_fusion.1) | copy-start | bytes 8644
  23.2 65.6 %copy-start.11 = (f32[1440]{0:T(1024)}, f32[1440]{0:T(1024)S(1)}, u32[]{:S(2)}) copy-start(f32[1440]{0:T(1024)S(1)} %iota_convert_fusion) | copy-start | bytes 17284
  74.8 14.0 %copy-start = (bf16[1,16,45,1440]{3,2,0,1:T(8,128)(2,1)}, bf16[1,16,45,1440]{3,2,0,1:T(8,128)(2,1)S(1)}, u32[]{:S(2)}) copy-start(bf16[1,16,45,1440]{3,2,0,1:T(8,128)(2,1)S(1)} %all-to-all-done) | copy-start | bytes 6220804
  184.8 9.0 copy-start.2
  205.7 0.8 copy-start.8
  205.7 1.7 copy-start.6
  205.7 1.7 copy-start.7
  205.7 2.5 copy-start.9
  205.7 4.0 copy-start.10
  360.8 162.4 %copy-start.4 = (f32[4,4096]{1,0:T(4,128)S(1)}, f32[4,4096]{1,0:T(4,128)}, u32[]{:S(2)}) copy-start(f32[4,4096]{1,0:T(4,128)} %squeeze.23) | copy-start | bytes 196612
  360.8 162.4 %copy-start.5 = (f32[4,4096]{1,0:T(4,128)S(1)}, f32[4,4096]{1,0:T(4,128)}, u32[]{:S(2)}) copy-start(f32[4,4096]{1,0:T(4,128)} %squeeze.24) | copy-start | bytes 196612
  714.6 4.2 copy-start.3
  723.7 10.8 %copy-start.1 = (bf16[1,16,45,1440]{3,2,0,1:T(8,128)(2,1)S(1)}, bf16[1,16,45,1440]{3,2,0,1:T(8,128)(2,1)}, u32[]{:S(2)}) copy-start(bf16[1,16,45,1440]{3,2,0,1:T(8,128)(2,1)} %copy-done) | copy-start | bytes 6220804
  726.4 61.1 %all-to-all-start.2 = ((bf16[1,16,45,1440]{3,2,0,1:T(8,128)(2,1)}), bf16[1,16,45,1440]{3,2,0,1:T(8,128)(2,1)}, u32[]{:S(2)}, u32[]{:S(2)}) async-start(bf16[1,16,45,1440]{3,2,0,1:T(8,128)(2,1)} %copy.37), calls=%async_computation.2 | async-start | bytes 4718592 | tf_op jit(solution)/shard_map/all_to_all | solution.py:96
  753.9 36.8 %copy-start.12 = (f32[1440]{0:T(1024)S(1)}, f32[1440]{0:T(1024)}, u32[]{:S(2)}) copy-start(f32[1440]{0:T(1024)} %copy-done.11) | copy-start | bytes 17284
  753.9 36.8 %copy-start.14 = (f32[720]{0:T(1024)S(1)}, f32[720]{0:T(1024)}, u32[]{:S(2)}) copy-start(f32[720]{0:T(1024)} %copy-done.13) | copy-start | bytes 8644
Sparse Core Ops, SparseCore 0:
  205.9 154.8 all-reduce.1
where the time goes:
time: 933 us; the launch traced here: 922 us
  other arithmetic  279 us (30%)
  local copies, waits for them, and re-layouts  240 us (26%)
  waiting for transfers between devices  234 us (25%)
  blocking collectives  110 us (12%)
  matrix products  23.7 us (3%)
  starting transfers between devices  17.6 us (2%)
  between operations  16.2 us (2%)
    scatter-add x4, other arithmetic, place_one_block(): return (field.at[rows_here].add(lines, mode='drop'), jnp.float32(0.0))  188 us
    psum x1, waiting for transfers between devices, shards(): total_field = lax.psum(partial_field, 'mem')  149 us
    gather x4, local copies, waits for them, and re-layouts, pick_one_block(): taken = flat_rows[rows_here]  118 us
    all_to_all x1, blocking collectives, shards(): lax.all_to_all(gradient_slab, 'tile', split_axis=2, concat_axis=1, tiled=...  55.3 us
    all_to_all x1, blocking collectives, shards(): lax.all_to_all(spread_slab, 'tile', split_axis=2, concat_axis=1, tiled=True)  55.2 us
    all_to_all x1, waiting for transfers between devices, shards(): lax.all_to_all(alpha, 'tile', split_axis=1, concat_axis=2, tiled=True)  51.6 us
    reduce_sum x4, other arithmetic, pick_one_block(): jnp.sum(jnp.where(counter[None, :] == cols_here[:, None], taken, 0.0), ax...  43.1 us
    unnamed x42, local copies, waits for them, and re-layouts  34.3 us
  transfers between devices with their start and end apart: 3, of which 3 were waited for; matrix products, arithmetic and copies ran while one was open for 3% of the time, Pallas kernels for 0%

commit v1 on v0

v1 whole, which is shorter than its diff:
```python
import functools

import jax
import jax.numpy as jnp
from jax import lax
from jax.experimental import pallas as pl
from jax.experimental.pallas import tpu as pltpu
from jax.sharding import PartitionSpec as P

LANES = 128
BLOCK = 256
RUN_BLOCKS = 5
RUN = RUN_BLOCKS * BLOCK
PLANES = 8
SEND_ROWS = 24
F32 = jnp.float32
BF16 = jnp.bfloat16
VMEM = pltpu.VMEM
SMEM = pltpu.SMEM


def round_up(value, step):
    return (value + step - 1) // step * step


def square_root(lengths, place, valid, extent, periodic):
    position = place.astype(F32)
    distance = jnp.abs(position[:, None] - position[None, :])
    if periodic:
        distance = jnp.minimum(distance, extent - distance)
    factor = (2.0 / jnp.pi) ** 0.25
    values = factor * jnp.exp(-((distance / lengths) ** 2)) / jnp.sqrt(lengths)
    values = jnp.where(valid[:, None] & valid[None, :], values, 0.0)
    return values.astype(BF16)


def split_three(value):
    first = value.astype(BF16).astype(F32)
    rest = value - first
    second = rest.astype(BF16).astype(F32)
    return first, second, rest - second


def look_up(table_ref, group, cells, lane_iota, line_iota):
    width = table_ref.shape[2]
    lines = jnp.concatenate(
        [table_ref[group, :, BLOCK * part : BLOCK * (part + 1)] for part in range(width // BLOCK)],
        axis=0,
    )
    results = []
    for cell in cells:
        chosen = jnp.where(lane_iota == (cell & (BLOCK - 1)), 1.0, 0.0).astype(BF16)
        found = jnp.dot(lines, chosen, preferred_element_type=F32)
        results.append(
            jnp.sum(jnp.where(line_iota == (cell >> 8), found, 0.0), axis=0, keepdims=True)
        )
    return results


def run_cells(run_ref, group):
    return [run_ref[group, part : part + 1, :].astype(jnp.int32) for part in range(RUN_BLOCKS)]


def pack_kernel(
    scalar_ref, level_ref, cell_ref, weight_ref, innov_ref, table_ref, send_out, target_ref, plane_ref, total_ref
):
    levels, rows, width = table_ref.shape
    lines = level_ref.shape[0]
    places = levels * RUN_BLOCKS
    count = scalar_ref[0]
    first_rank = scalar_ref[1] * RUN
    slot = lax.broadcasted_iota(jnp.int32, (lines, LANES), 0) * LANES + lax.broadcasted_iota(
        jnp.int32, (lines, LANES), 1
    )
    level = jnp.where(slot < count, level_ref[...], levels)
    row_at = lax.broadcasted_iota(jnp.int32, (LANES, LANES), 0)
    lane_at = lax.broadcasted_iota(jnp.int32, (LANES, LANES), 1)
    upper = jnp.where(row_at <= lane_at, 1.0, 0.0).astype(BF16)
    ones = jnp.ones((LANES, LANES), BF16)
    before = jnp.where(
        lax.broadcasted_iota(jnp.int32, (lines, lines), 1)
        < lax.broadcasted_iota(jnp.int32, (lines, lines), 0),
        1.0,
        0.0,
    ).astype(BF16)
    rank = jnp.zeros((lines, LANES), F32)
    longest = jnp.zeros((1, LANES), F32)
    for index in range(levels):
        mask = level == index
        flags = jnp.where(mask, 1.0, 0.0).astype(BF16)
        inside = jnp.dot(flags, upper, preferred_element_type=F32)
        line_total = jnp.dot(flags, ones, preferred_element_type=F32)
        ahead = jnp.dot(before, line_total.astype(BF16), preferred_element_type=F32)
        rank = jnp.where(mask, ahead + inside - 1.0, rank)
        longest = jnp.maximum(longest, ahead[lines - 1 :, :] + line_total[lines - 1 :, :])
    place = rank.astype(jnp.int32) - first_rank
    kept = (level < levels) & (place >= 0) & (place < RUN)
    target_ref[...] = jnp.where(kept, level * RUN + place, -1)
    cell = cell_ref[...]
    plane_ref[0] = (cell & (BLOCK - 1)).astype(F32)
    plane_ref[1] = ((cell >> 8) - BLOCK // 2).astype(F32)
    for index, part in enumerate(split_three(weight_ref[...])):
        plane_ref[2 + index] = part
    for index, part in enumerate(split_three(innov_ref[...])):
        plane_ref[5 + index] = part
    total_ref[...] = jnp.zeros_like(total_ref)
    block_at = lax.broadcasted_iota(jnp.int32, (places, BLOCK), 0)
    lane_iota = lax.broadcasted_iota(jnp.int32, (BLOCK, BLOCK), 0)

    def pair_of(ref, index):
        return jnp.concatenate([ref[pl.ds(2 * index, 1), :], ref[pl.ds(2 * index + 1, 1), :]], axis=1)

    def place_block(index, carry):
        target = pair_of(target_ref, index)
        target_block = block_at == (target >> 8)
        target_lane = jnp.where(lane_iota == (target & (BLOCK - 1)), 1.0, 0.0).astype(BF16)
        parts = [
            jnp.where(target_block, pair_of(plane_ref.at[plane], index), 0.0).astype(BF16)
            for plane in range(PLANES)
        ]
        total_ref[...] += lax.dot_general(
            jnp.concatenate(parts, axis=0),
            target_lane,
            (((1,), (1,)), ((), ())),
            preferred_element_type=F32,
        )
        return carry

    lax.fori_loop(0, lines // 2, place_block, 0)
    planes = [total_ref[places * plane : places * (plane + 1), :] for plane in range(PLANES)]
    cell_sorted = (planes[1] + float(BLOCK // 2)) * float(BLOCK) + planes[0]
    weight_sorted = planes[2] + planes[3] + planes[4]
    innov_sorted = planes[5] + planes[6] + planes[7]
    tail = jnp.concatenate([longest] * (BLOCK // LANES), axis=1)
    for index in range(levels):
        run = slice(RUN_BLOCKS * index, RUN_BLOCKS * (index + 1))
        send_out[index, 0:RUN_BLOCKS, :] = cell_sorted[run]
        send_out[index, RUN_BLOCKS : 2 * RUN_BLOCKS, :] = weight_sorted[run]
        send_out[index, 2 * RUN_BLOCKS : 3 * RUN_BLOCKS, :] = innov_sorted[run]
        send_out[index, 4 * RUN_BLOCKS : SEND_ROWS, :] = jnp.broadcast_to(
            tail, (SEND_ROWS - 4 * RUN_BLOCKS, BLOCK)
        )
    line_iota = lax.broadcasted_iota(jnp.int32, (rows * width // BLOCK, BLOCK), 0)

    def one_level(index, carry):
        found = look_up(table_ref, index, run_cells(send_out, index), lane_iota, line_iota)
        for part in range(RUN_BLOCKS):
            send_out[index, 3 * RUN_BLOCKS + part : 3 * RUN_BLOCKS + part + 1, :] = found[part]
        return carry

    lax.fori_loop(0, levels, one_level, 0)


def pack_slots(scalars, level, cell, weight, innov, table):
    lines = level.shape[0]
    levels = table.shape[0]
    places = levels * RUN_BLOCKS
    whole = pl.BlockSpec(memory_space=VMEM)
    return pl.pallas_call(
        pack_kernel,
        out_shape=jax.ShapeDtypeStruct((levels, SEND_ROWS, BLOCK), F32),
        in_specs=[pl.BlockSpec(memory_space=SMEM)] + [whole] * 5,
        out_specs=whole,
        scratch_shapes=[
            VMEM((lines, LANES), jnp.int32),
            VMEM((PLANES, lines, LANES), F32),
            VMEM((PLANES * places, BLOCK), F32),
        ],
        compiler_params=pltpu.CompilerParams(vmem_limit_bytes=24 << 20),
        cost_estimate=pl.CostEstimate(flops=25 * 10**9, bytes_accessed=4 << 20, transcendentals=0),
        name="pack_slots",
    )(scalars, level, cell, weight, innov, table)


def term_kernel(table_ref, run_ref, term_out):
    groups, rows, width = table_ref.shape
    lane_iota = lax.broadcasted_iota(jnp.int32, (BLOCK, BLOCK), 0)
    line_iota = lax.broadcasted_iota(jnp.int32, (rows * width // BLOCK, BLOCK), 0)

    def one_group(group, carry):
        found = look_up(table_ref, group, run_cells(run_ref, group), lane_iota, line_iota)
        for part in range(RUN_BLOCKS):
            row = 3 * RUN_BLOCKS + part
            term_out[pl.ds(group * RUN_BLOCKS + part, 1), :] = (
                found[part] * run_ref[group, row : row + 1, :]
            )
        return carry

    lax.fori_loop(0, groups, one_group, 0)


def slot_terms(table, runs):
    groups = table.shape[0]
    whole = pl.BlockSpec(memory_space=VMEM)
    return pl.pallas_call(
        term_kernel,
        out_shape=jax.ShapeDtypeStruct((groups * RUN_BLOCKS, BLOCK), F32),
        in_specs=[whole, whole],
        out_specs=whole,
        compiler_params=pltpu.CompilerParams(vmem_limit_bytes=24 << 20),
        cost_estimate=pl.CostEstimate(flops=4 * 10**9, bytes_accessed=3 << 20, transcendentals=0),
        name="slot_terms",
    )(table, runs)


def add_kernel(run_ref, model_ref, field_out):
    groups, rows, width = field_out.shape
    parts = width // BLOCK
    lane_iota = lax.broadcasted_iota(jnp.int32, (BLOCK, RUN), 0)
    line_iota = lax.broadcasted_iota(jnp.int32, (rows * parts, RUN), 0)

    def one_group(group, carry):
        def row_of(first):
            return jnp.concatenate(
                [run_ref[group, first + part : first + part + 1, :] for part in range(RUN_BLOCKS)],
                axis=1,
            )

        cell = row_of(0).astype(jnp.int32)
        model = jnp.concatenate(
            [model_ref[pl.ds(group * RUN_BLOCKS + part, 1), :] for part in range(RUN_BLOCKS)], axis=1
        )
        weighted = row_of(RUN_BLOCKS) * (model - row_of(2 * RUN_BLOCKS))
        value = row_of(3 * RUN_BLOCKS) * weighted
        lines = jnp.where(line_iota == (cell >> 8), value, 0.0).astype(BF16)
        chosen = jnp.where(lane_iota == (cell & (BLOCK - 1)), 1.0, 0.0).astype(BF16)
        total = lax.dot_general(
            lines, chosen, (((1,), (1,)), ((), ())), preferred_element_type=F32
        )
        for part in range(parts):
            field_out[group, :, BLOCK * part : BLOCK * (part + 1)] = total[
                rows * part : rows * (part + 1), :
            ].astype(field_out.dtype)
        return carry

    lax.fori_loop(0, groups, one_group, 0)


def add_slots(runs, model, rows, width, dtype):
    groups = runs.shape[0]
    whole = pl.BlockSpec(memory_space=VMEM)
    return pl.pallas_call(
        add_kernel,
        out_shape=jax.ShapeDtypeStruct((groups, rows, width), dtype),
        in_specs=[whole, whole],
        out_specs=whole,
        compiler_params=pltpu.CompilerParams(vmem_limit_bytes=24 << 20),
        cost_estimate=pl.CostEstimate(flops=4 * 10**9, bytes_accessed=3 << 20, transcendentals=0),
        name="add_slots",
    )(runs, model)


def localize(values, lat_root, lon_root):
    zonal = jnp.dot(values, lon_root, preferred_element_type=F32).astype(BF16)
    return jnp.dot(lat_root, zonal, preferred_element_type=F32)


def sum_members(value):
    members = lax.axis_size("mem")
    step = 1
    while step < members:
        value = value + lax.ppermute(value, "mem", [(i, i ^ step) for i in range(members)])
        step *= 2
    return value


def exchange(value):
    return lax.all_to_all(value, "tile", split_axis=0, concat_axis=0, tiled=True)


def shards(
    alpha,
    perturbation,
    lon_scale,
    lat_scale,
    obs_level,
    obs_row,
    obs_col,
    obs_count,
    innovation,
    obs_weight,
):
    levels, rows, columns = alpha.shape[1:]
    tiles = lax.axis_size("tile")
    level = lax.axis_index("tile")
    slots = obs_level.shape[1]
    pad_rows = round_up(rows, 16)
    width = round_up(columns, BLOCK)
    padding = ((0, 0), (0, pad_rows - rows), (0, width - columns))

    alpha_slab = exchange(alpha[0])

    as_lines = lambda value: value.reshape(slots // LANES, LANES)
    column = as_lines(obs_col)
    cell = ((column >> 8) * pad_rows + as_lines(obs_row)) * BLOCK + (column & (BLOCK - 1))
    pert_table = jnp.pad(perturbation[0], padding)

    def packed_chunk(chunk):
        scalars = jnp.stack([obs_count[0], chunk])
        return pack_slots(
            scalars,
            as_lines(obs_level),
            cell,
            as_lines(obs_weight),
            as_lines(innovation),
            pert_table,
        )

    alpha_slab, packed = lax.optimization_barrier((alpha_slab, packed_chunk(jnp.int32(0))))
    runs = exchange(packed)
    longest = jnp.max(runs[:, SEND_ROWS - 1, 0]).astype(jnp.int32)

    column_at = jnp.arange(width)
    lon_root = square_root(
        lax.dynamic_index_in_dim(lon_scale, level, keepdims=False),
        column_at,
        column_at < columns,
        columns,
        True,
    )
    line = jnp.arange(tiles * pad_rows)
    row_in_band = line % pad_rows
    lat_root = square_root(
        lax.dynamic_index_in_dim(lat_scale, level, keepdims=False),
        (line // pad_rows) * rows + row_in_band,
        row_in_band < rows,
        rows * tiles,
        False,
    )
    lon_root, lat_root = lax.optimization_barrier((lon_root, lat_root))

    padded = jnp.pad(alpha_slab, padding).reshape(tiles * pad_rows, width)
    spread = localize(padded, lat_root, lon_root).astype(BF16).reshape(tiles, pad_rows, width)

    def chunk_field(chunk_run, dtype):
        model = sum_members(slot_terms(spread, chunk_run))
        return add_slots(chunk_run, model, pad_rows, width, dtype)

    def one_run():
        return chunk_field(runs, BF16)

    def many_runs():
        def one_chunk(chunk, field):
            return field + chunk_field(exchange(packed_chunk(chunk)), F32)

        start = jnp.zeros((tiles, pad_rows, width), F32)
        return lax.fori_loop(0, (longest + RUN - 1) // RUN, one_chunk, start).astype(BF16)

    sensitive = lax.cond(longest > RUN, many_runs, one_run)
    back = localize(sensitive.reshape(tiles * pad_rows, width), lat_root, lon_root)
    back = back.reshape(tiles, pad_rows, width)[:, :rows, :columns]
    gradient = (alpha_slab.astype(F32) + back).astype(BF16)
    return exchange(gradient)[None]


def solution(mesh):
    in_specs = (
        P("mem", None, "tile", None),
        P("mem", None, "tile", None),
        P(),
        P(),
        P("tile", None),
        P("tile", None),
        P("tile", None),
        P("tile"),
        P("tile", None),
        P("tile", None),
    )
    out_specs = P("mem", None, "tile", None)
    return jax.shard_map(shards, mesh=mesh, in_specs=in_specs, out_specs=out_specs, check_vma=False)
```

time: 933 us -> 201 us (0.22); the launches traced: 922 us -> 200 us
  other arithmetic: 279 us -> 13.4 us
  local copies, waits for them, and re-layouts: 240 us -> 15.8 us
  waiting for transfers between devices: 234 us -> 21.2 us
  blocking collectives: 110 us -> 58 us
  Pallas kernels: 0 us -> 44.6 us
  between operations: 16.2 us -> 2.84 us
    scatter-add x4 -> x0, other arithmetic: 188 us -> none  [place_one_block(): return (field.at[rows_here].add(lines, mode='drop'), jnp.float32(0.0))]
    psum x1 -> x0, waiting for transfers between devices: 149 us -> none  [shards(): total_field = lax.psum(partial_field, 'mem')]
    gather x4 -> x0, local copies, waits for them, and re-layouts: 118 us -> none  [pick_one_block(): taken = flat_rows[rows_here]]
    all_to_all x2, waiting for transfers between devices: 85.1 us -> 11 us  [exchange(): lax.all_to_all(value, 'tile', split_axis=0, concat_axis=0, tiled=True)]
    all_to_all x2 -> x1, blocking collectives: 110 us -> 58 us  [exchange(): lax.all_to_all(value, 'tile', split_axis=0, concat_axis=0, tiled=True)]
    pallas_call x0 -> x3, Pallas kernels: none -> 44.6 us  [the longest x1 29.2 us: pack_slots(): pl.pallas_call(pack_kernel, out_shape=jax.ShapeDtypeStruct((levels, SEND_...]
    convert_element_type x5 -> x0, local copies, waits for them, and re-layouts: 43.5 us -> none  [the longest x2 19.4 us: shards(): alpha_slab.astype(jnp.float32)]
    reduce_sum x4 -> x0, other arithmetic: 43.1 us -> none  [pick_one_block(): jnp.sum(jnp.where(counter[None, :] == cols_here[:, None], taken, 0.0), ax...]
  transfers between devices with their start and end apart: 3 -> 6, of which waited for: 3 -> 6; matrix products, arithmetic and copies ran while one was open for 3% -> 12% of each run, Pallas kernels for 0% -> 15%
where the time goes in v1:
time: 201 us; the launch traced here: 200 us
  blocking collectives  58 us (29%)
  Pallas kernels  44.6 us (22%)
  starting transfers between devices  24 us (12%)
  waiting for transfers between devices  21.2 us (11%)
  matrix products  20.1 us (10%)
  local copies, waits for them, and re-layouts  15.8 us (8%)
  other arithmetic  13.4 us (7%)
  between operations  2.84 us (1%)
    all_to_all x1, blocking collectives, exchange(): lax.all_to_all(value, 'tile', split_axis=0, concat_axis=0, tiled=True)  58 us
    pallas_call x1, Pallas kernels, pack_slots(): pl.pallas_call(pack_kernel, out_shape=jax.ShapeDtypeStruct((levels, SEND_...  29.2 us
    dot_general x2, matrix products, localize(): return jnp.dot(lat_root, zonal, preferred_element_type=F32)  20.1 us
    all_to_all x2, starting transfers between devices, exchange(): lax.all_to_all(value, 'tile', split_axis=0, concat_axis=0, tiled=True)  16.2 us
    all_to_all x2, waiting for transfers between devices, exchange(): lax.all_to_all(value, 'tile', split_axis=0, concat_axis=0, tiled=True)  11 us
    ppermute x4, waiting for transfers between devices, sum_members(): lax.ppermute(value, 'mem', [(i, i ^ step) for i in range(members)])  10.2 us
    unnamed x28, local copies, waits for them, and re-layouts  10 us
    convert_element_type x2, other arithmetic, square_root(): return values.astype(BF16)  7.95 us
  transfers between devices with their start and end apart: 6, of which 6 were waited for; matrix products, arithmetic and copies ran while one was open for 12% of the time, Pallas kernels for 15%

profile of v1, /device:TPU:32, one launch (start us, length us, event | category | flops | bytes accessed | tf_op | source)
XLA Modules:
  0.0 200.1 jit_solution(6268092006189224835)
XLA Ops:
  0.0 4.3 %copy.19 = bf16[1,16,45,1440]{3,2,1,0:T(8,128)(2,1)} copy(bf16[1,16,45,1440]{3,1,2,0:T(8,128)(2,1)} %param.14) | data formatting | bytes 4147200 | tf_op args[0]
  4.3 9.6 %all-to-all-start.1 = ((bf16[16,45,1440]{2,1,0:T(8,128)(2,1)}), bf16[16,45,1440]{2,1,0:T(8,128)(2,1)S(1)}, u32[]{:S(2)}, u32[]{:S(2)}) async-start(bf16[16,45,1440]{2,1,0:T(8,128)(2,1)} %bitcast.36), calls=%async_computation.1 | async-start | bytes 4718592 | tf_op jit(solution)/shard_map/all_to_all | solution.py:268
  15.3 6.4 %fusion.7 = bf16[1536,1536]{1,0:T(8,128)(2,1)} fusion(f32[]{:T(128)S(6)} %sqrt.6, f32[]{:T(128)} %bitcast.12, f32[1536]{0:T(1024)S(1)} %iota_convert_fusion, pred[1536]{0:T(1024)(128)(4,1)S(1)} %iota_compare_fusion), kind=kLoop, calls=%fused_computation.9 | loop fusion | flops 28311552 | bytes 4726280 | tf_op jit(solution)/shard_map/convert_element_type | solution.py:34
  24.3 2.8 %copy.18 = bf16[1,16,45,1440]{3,2,1,0:T(8,128)(2,1)S(1)} copy(bf16[1,16,45,1440]{3,1,2,0:T(8,128)(2,1)} %param.15) | data formatting | bytes 4147200 | tf_op args[1]
  27.2 1.6 select_convert_fusion
  30.6 29.2 %pack_slots.2 = f32[16,24,256]{2,1,0:T(8,128)} custom-call(s32[2]{0:T(128)S(1)} %pad_add_fusion.1.scalar_ref, s32[128,128]{1,0:T(8,128)S(1)} %bitcast.43, s32[128,128]{1,0:T(8,128)S(1)} %bitcast.42, f32[128,128]{1,0:T(8,128)S(1)} %bitcast.45, f32[128,128]{1,0:T(8,128)S(1)} %bitcast.47, bf16[16,48,1536]{2,1,0:T(8,128)(2,1)S(1)} %pad.7.table_ref), custom_call_target="tpu_custom_call" | custom-call | flops 24999999488 | bytes 4194304 | tf_op jit(solution)/shard_map/pack_slots/pallas_call | solution.py:159
  59.8 8.7 %all-to-all-done.1 = bf16[16,45,1440]{2,1,0:T(8,128)(2,1)S(1)} async-done(((bf16[16,45,1440]{2,1,0:T(8,128)(2,1)}), bf16[16,45,1440]{2,1,0:T(8,128)(2,1)S(1)}, u32[]{:S(2)}, u32[]{:S(2)}) %all-to-all-start.1) | async-done | bytes 2073632 | tf_op jit(solution)/shard_map/all_to_all | solution.py:268
  68.5 6.6 %all-to-all-start.2 = ((f32[16,24,256]{2,1,0:T(8,128)}), f32[16,24,256]{2,1,0:T(8,128)}, u32[]{:S(2)}, u32[]{:S(2)}) async-start(f32[16,24,256]{2,1,0:T(8,128)} %pack_slots.2), calls=%async_computation.2 | async-start | bytes 786432 | tf_op jit(solution)/shard_map/all_to_all | solution.py:268
  75.0 1.7 pad.8
  76.7 8.7 %convolution_convert_fusion.1 = bf16[768,1536]{1,0:T(8,128)(2,1)S(1)} fusion(bf16[768,768]{1,0:T(8,128)(2,1)S(1)} %select_convert_fusion, bf16[768,1536]{1,0:T(8,128)(2,1)} %bitcast.40, bf16[1536,1536]{1,0:T(8,128)(2,1)} %fusion.7), kind=kOutput, calls=%fused_computation.13 | convolution fusion | flops 5438177280 | bytes 10616832 | tf_op jit(solution)/shard_map/dot_general | solution.py:255
  85.4 2.4 %all-to-all-done.2 = f32[16,24,256]{2,1,0:T(8,128)} async-done(((f32[16,24,256]{2,1,0:T(8,128)}), f32[16,24,256]{2,1,0:T(8,128)}, u32[]{:S(2)}, u32[]{:S(2)}) %all-to-all-start.2) | async-done | bytes 393248 | tf_op jit(solution)/shard_map/all_to_all | solution.py:268
  89.9 33.7 %conditional.1 = (bf16[768,1536]{1,0:T(8,128)(2,1)S(1)}) conditional(s32[]{:T(128)} %convert_element_type.61, (bf16[16,48,1536]{2,1,0:T(8,128)(2,1)S(1)}, f32[16,24,256]{2,1,0:T(8,128)}) %tuple.43, (s32[]{:T(128)}, s32[1]{0:T(128)}, s32[1,16384]{1,0:T(1,128)}, f32[1,16384]{1,0:T(1,128)}, f32[1,16384]{1,0:T(1,128)}, /*index=5*/s32[128,128]{1,0:T(8,128)}, ...), branch_computations={%region_1.2_spmd, %region_2.5_spmd} | conditional | flops 33002440704 | bytes 68879016 | solution.py:349
  89.9 7.8 %slot_terms.2 = f32[80,256]{1,0:T(8,128)S(1)} custom-call(bf16[16,48,1536]{2,1,0:T(8,128)(2,1)S(1)} %get-tuple-element.70.table_ref, f32[16,24,256]{2,1,0:T(8,128)} %get-tuple-element.69.run_ref), custom_call_target="tpu_custom_call" | custom-call | flops 4000000000 | bytes 3145728 | tf_op jit(solution)/shard_map/cond/branch_0_fun/slot_terms/pallas_call | solution.py:195
  99.1 1.7 collective-permute-start.1
  100.8 2.9 %collective-permute-done.1 = f32[80,256]{1,0:T(8,128)S(1)} collective-permute-done((f32[80,256]{1,0:T(8,128)S(1)}, f32[80,256]{1,0:T(8,128)S(1)}, u32[]{:S(2)}, u32[]{:S(2)}) %collective-permute-start.1) | collective-permute-done | bytes 81952 | tf_op jit(solution)/shard_map/cond/branch_0_fun/ppermute | solution.py:262
  103.7 3.3 %collective-permute-start.2 = (f32[80,256]{1,0:T(8,128)S(1)}, f32[80,256]{1,0:T(8,128)S(1)}, u32[]{:S(2)}, u32[]{:S(2)}) collective-permute-start(f32[80,256]{1,0:T(8,128)S(1)} %add.76), channel_id=1, source_target_pairs={{0,64},{16,80},{32,96},{48,112},{64,0},{80,16},{96,32},{112,48},{1... | collective-permute-start | bytes 245768 | tf_op jit(solution)/shard_map/cond/branch_0_fun/ppermute | solution.py:262
  107.0 2.8 %collective-permute-done.2 = f32[80,256]{1,0:T(8,128)S(1)} collective-permute-done((f32[80,256]{1,0:T(8,128)S(1)}, f32[80,256]{1,0:T(8,128)S(1)}, u32[]{:S(2)}, u32[]{:S(2)}) %collective-permute-start.2) | collective-permute-done | bytes 81952 | tf_op jit(solution)/shard_map/cond/branch_0_fun/ppermute | solution.py:262
  109.8 2.8 %collective-permute-start.3 = (f32[80,256]{1,0:T(8,128)S(1)}, f32[80,256]{1,0:T(8,128)S(1)}, u32[]{:S(2)}, u32[]{:S(2)}) collective-permute-start(f32[80,256]{1,0:T(8,128)S(1)} %add.77), channel_id=1, source_target_pairs={{0,128},{16,144},{32,160},{48,176},{64,192},{80,208},{96,224},{112... | collective-permute-start | bytes 245768 | tf_op jit(solution)/shard_map/cond/branch_0_fun/ppermute | solution.py:262
  112.6 3.2 %collective-permute-done.3 = f32[80,256]{1,0:T(8,128)S(1)} collective-permute-done((f32[80,256]{1,0:T(8,128)S(1)}, f32[80,256]{1,0:T(8,128)S(1)}, u32[]{:S(2)}, u32[]{:S(2)}) %collective-permute-start.3) | collective-permute-done | bytes 81952 | tf_op jit(solution)/shard_map/cond/branch_0_fun/ppermute | solution.py:262
  115.8 7.6 %add_slots.2 = bf16[16,48,1536]{2,1,0:T(8,128)(2,1)S(1)} custom-call(f32[16,24,256]{2,1,0:T(8,128)} %get-tuple-element.69.run_ref, f32[80,256]{1,0:T(8,128)S(1)} %add.78.model_ref), custom_call_target="tpu_custom_call" | custom-call | flops 4000000000 | bytes 3145728 | tf_op jit(solution)/shard_map/cond/branch_0_fun/add_slots/pallas_call | solution.py:242
  125.0 11.4 %fusion.9 = f32[768,1536]{1,0:T(8,128)} fusion(bf16[768,768]{1,0:T(8,128)(2,1)} %copy-done.4, bf16[768,1536]{1,0:T(8,128)(2,1)} %copy-done.19, bf16[1536,1536]{1,0:T(8,128)(2,1)} %fusion.7), kind=kOutput, calls=%fused_computation.18 | convolution fusion | flops 5436997632 | bytes 12976128 | tf_op jit(solution)/shard_map/dot_general | solution.py:255
  136.4 3.1 %fusion.8 = bf16[16,45,1440]{2,1,0:T(8,128)(2,1)S(1)} fusion(f32[16,48,1536]{2,1,0:T(8,128)} %bitcast.39, bf16[16,45,1440]{2,1,0:T(8,128)(2,1)S(1)} %copy-done.1), kind=kLoop, calls=%fused_computation.11 | loop fusion | flops 3110400 | bytes 8294400 | tf_op jit(solution)/shard_map/convert_element_type | solution.py:352
  139.5 58.0 %all_to_all.21 = bf16[16,45,1440]{2,1,0:T(8,128)(2,1)S(1)} all-to-all(bf16[16,45,1440]{2,1,0:T(8,128)(2,1)S(1)} %fusion.8), channel_id=1, replica_groups=mesh['mem'=16,'tile'=16] {'tile'}, dimensions={0} | all-to-all | bytes 4147200 | tf_op jit(solution)/shard_map/all_to_all | solution.py:268
  197.5 2.6 %copy.15 = bf16[1,16,45,1440]{3,1,2,0:T(8,128)(2,1)} copy(bf16[1,16,45,1440]{3,2,1,0:T(8,128)(2,1)S(1)} %bitcast.38) | data formatting | bytes 4147200 | tf_op jit(solution)/shard_map/broadcast_in_dim | solution.py:353
  (42 shorter events, 8.0 us)
Async XLA Ops:
  4.3 9.7 %copy-start.15 = (f32[16]{0:T(128)S(1)}, f32[16]{0:T(128)}, u32[]{:S(2)}) copy-start(f32[16]{0:T(128)} %param.16) | copy-start | bytes 196
  4.3 64.2 %all-to-all-start.1 = ((bf16[16,45,1440]{2,1,0:T(8,128)(2,1)}), bf16[16,45,1440]{2,1,0:T(8,128)(2,1)S(1)}, u32[]{:S(2)}, u32[]{:S(2)}) async-start(bf16[16,45,1440]{2,1,0:T(8,128)(2,1)} %bitcast.36), calls=%async_computation.1 | async-start | bytes 4718592 | tf_op jit(solution)/shard_map/all_to_all | solution.py:268
  15.3 6.4 %copy-start.5 = (s32[1,16384]{1,0:T(1,128)S(1)}, s32[1,16384]{1,0:T(1,128)}, u32[]{:S(2)}) copy-start(s32[1,16384]{1,0:T(1,128)} %param.20) | copy-start | bytes 196612
  15.3 6.4 %copy-start.6 = (s32[1,16384]{1,0:T(1,128)S(1)}, s32[1,16384]{1,0:T(1,128)}, u32[]{:S(2)}) copy-start(s32[1,16384]{1,0:T(1,128)} %param.19) | copy-start | bytes 196612
  15.3 7.8 %copy-start.16 = (f32[16]{0:T(128)S(1)}, f32[16]{0:T(128)}, u32[]{:S(2)}) copy-start(f32[16]{0:T(128)} %param.17) | copy-start | bytes 196
  28.8 47.9 %copy-start.4 = (bf16[768,768]{1,0:T(8,128)(2,1)}, bf16[768,768]{1,0:T(8,128)(2,1)S(1)}, u32[]{:S(2)}) copy-start(bf16[768,768]{1,0:T(8,128)(2,1)S(1)} %select_convert_fusion) | copy-start | bytes 3538948
  28.8 1.8 copy-start.7
  28.8 1.8 copy-start.9
  28.9 1.8 copy-start.11
  28.9 1.7 copy-start.13
  29.2 1.4 copy-start.2
  68.5 8.3 %copy-start = (bf16[16,45,1440]{2,1,0:T(8,128)(2,1)}, bf16[16,45,1440]{2,1,0:T(8,128)(2,1)S(1)}, u32[]{:S(2)}) copy-start(bf16[16,45,1440]{2,1,0:T(8,128)(2,1)S(1)} %all-to-all-done.1) | copy-start | bytes 6220804
  68.5 19.3 %all-to-all-start.2 = ((f32[16,24,256]{2,1,0:T(8,128)}), f32[16,24,256]{2,1,0:T(8,128)}, u32[]{:S(2)}, u32[]{:S(2)}) async-start(f32[16,24,256]{2,1,0:T(8,128)} %pack_slots.2), calls=%async_computation.2 | async-start | bytes 786432 | tf_op jit(solution)/shard_map/all_to_all | solution.py:268
  97.7 1.4 collective-permute-start
  99.1 4.6 %collective-permute-start.1 = (f32[80,256]{1,0:T(8,128)S(1)}, f32[80,256]{1,0:T(8,128)S(1)}, u32[]{:S(2)}, u32[]{:S(2)}) collective-permute-start(f32[80,256]{1,0:T(8,128)S(1)} %add.75), channel_id=1, source_target_pairs={{0,32},{16,48},{32,0},{48,16},{64,96},{80,112},{96,64},{112,80},{1... | collective-permute-start | bytes 245768 | tf_op jit(solution)/shard_map/cond/branch_0_fun/ppermute | solution.py:262
  103.7 6.0 %collective-permute-start.2 = (f32[80,256]{1,0:T(8,128)S(1)}, f32[80,256]{1,0:T(8,128)S(1)}, u32[]{:S(2)}, u32[]{:S(2)}) collective-permute-start(f32[80,256]{1,0:T(8,128)S(1)} %add.76), channel_id=1, source_target_pairs={{0,64},{16,80},{32,96},{48,112},{64,0},{80,16},{96,32},{112,48},{1... | collective-permute-start | bytes 245768 | tf_op jit(solution)/shard_map/cond/branch_0_fun/ppermute | solution.py:262
  109.8 6.0 %collective-permute-start.3 = (f32[80,256]{1,0:T(8,128)S(1)}, f32[80,256]{1,0:T(8,128)S(1)}, u32[]{:S(2)}, u32[]{:S(2)}) collective-permute-start(f32[80,256]{1,0:T(8,128)S(1)} %add.77), channel_id=1, source_target_pairs={{0,128},{16,144},{32,160},{48,176},{64,192},{80,208},{96,224},{112... | collective-permute-start | bytes 245768 | tf_op jit(solution)/shard_map/cond/branch_0_fun/ppermute | solution.py:262
  123.6 1.4 copy-start.19
  125.0 11.4 %copy-start.1 = (bf16[16,45,1440]{2,1,0:T(8,128)(2,1)S(1)}, bf16[16,45,1440]{2,1,0:T(8,128)(2,1)}, u32[]{:S(2)}) copy-start(bf16[16,45,1440]{2,1,0:T(8,128)(2,1)} %copy-done) | copy-start | bytes 6220804

commit v2 on v1

--- a/solution.py
+++ b/solution.py
@@ -9,10 +9,12 @@
 
 LANES = 128
 BLOCK = 256
-RUN_BLOCKS = 5
-RUN = RUN_BLOCKS * BLOCK
+RUN_ROWS = 9
+RUN = RUN_ROWS * LANES
 PLANES = 8
-SEND_ROWS = 24
+SEND_ROWS = 40
+ROW_STRIDE = 64
+UNROLL = 4
 F32 = jnp.float32
 BF16 = jnp.bfloat16
 VMEM = pltpu.VMEM
@@ -41,24 +43,49 @@
     return first, second, rest - second
 
 
-def look_up(table_ref, group, cells, lane_iota, line_iota):
-    width = table_ref.shape[2]
+def small_float(value):
+    return value.astype(F32).astype(BF16)
+
+
+def run_pieces(run_ref, group, first):
+    rows = [run_ref[group, first + row : first + row + 1, :] for row in range(RUN_ROWS)]
+    pieces = [
+        jnp.concatenate(rows[row : row + 2], axis=1) for row in range(0, RUN_ROWS - 1, 2)
+    ]
+    return pieces + rows[RUN_ROWS - 1 :] if RUN_ROWS % 2 else pieces
+
+
+def look_up(table_ref, group, cells, lane_index, row_index):
+    rows, width = table_ref.shape[1:]
+    parts = width // BLOCK
     lines = jnp.concatenate(
-        [table_ref[group, :, BLOCK * part : BLOCK * (part + 1)] for part in range(width // BLOCK)],
-        axis=0,
+        [table_ref[group, :, BLOCK * part : BLOCK * (part + 1)] for part in range(parts)], axis=0
     )
     results = []
-    for cell in cells:
-        chosen = jnp.where(lane_iota == (cell & (BLOCK - 1)), 1.0, 0.0).astype(BF16)
+    for piece in cells:
+        cell = piece.astype(jnp.int32)
+        lanes = cell.shape[1]
+        chosen = jnp.where(
+            lane_index[:, :lanes] == small_float(cell & (BLOCK - 1)), jnp.ones((), BF16), jnp.zeros((), BF16)
+        )
         found = jnp.dot(lines, chosen, preferred_element_type=F32)
-        results.append(
-            jnp.sum(jnp.where(line_iota == (cell >> 8), found, 0.0), axis=0, keepdims=True)
-        )
+        part_of = cell >> 14
+        kept = found[0:rows]
+        for part in range(1, parts):
+            kept = jnp.where(part_of == part, found[rows * part : rows * (part + 1)], kept)
+        row_of = (cell >> 8) & (ROW_STRIDE - 1)
+        value = jnp.sum(
+            jnp.where(row_index[:, :lanes] == row_of, kept, 0.0), axis=0, keepdims=True
+        )
+        for half in range(lanes // LANES):
+            results.append(value[:, LANES * half : LANES * (half + 1)])
     return results
 
 
-def run_cells(run_ref, group):
-    return [run_ref[group, part : part + 1, :].astype(jnp.int32) for part in range(RUN_BLOCKS)]
+def look_up_indices(rows):
+    lane_index = small_float(lax.broadcasted_iota(jnp.int32, (BLOCK, BLOCK), 0))
+    row_index = lax.broadcasted_iota(jnp.int32, (rows, BLOCK), 0)
+    return lane_index, row_index
 
 
 def pack_kernel(
@@ -66,7 +93,7 @@
 ):
     levels, rows, width = table_ref.shape
     lines = level_ref.shape[0]
-    places = levels * RUN_BLOCKS
+    places = levels * RUN // BLOCK
     count = scalar_ref[0]
     first_rank = scalar_ref[1] * RUN
     slot = lax.broadcasted_iota(jnp.int32, (lines, LANES), 0) * LANES + lax.broadcasted_iota(
@@ -131,34 +158,37 @@
     cell_sorted = (planes[1] + float(BLOCK // 2)) * float(BLOCK) + planes[0]
     weight_sorted = planes[2] + planes[3] + planes[4]
     innov_sorted = planes[5] + planes[6] + planes[7]
-    tail = jnp.concatenate([longest] * (BLOCK // LANES), axis=1)
     for index in range(levels):
-        run = slice(RUN_BLOCKS * index, RUN_BLOCKS * (index + 1))
-        send_out[index, 0:RUN_BLOCKS, :] = cell_sorted[run]
-        send_out[index, RUN_BLOCKS : 2 * RUN_BLOCKS, :] = weight_sorted[run]
-        send_out[index, 2 * RUN_BLOCKS : 3 * RUN_BLOCKS, :] = innov_sorted[run]
-        send_out[index, 4 * RUN_BLOCKS : SEND_ROWS, :] = jnp.broadcast_to(
-            tail, (SEND_ROWS - 4 * RUN_BLOCKS, BLOCK)
-        )
-    line_iota = lax.broadcasted_iota(jnp.int32, (rows * width // BLOCK, BLOCK), 0)
+        for row in range(RUN_ROWS):
+            line, half = divmod(index * RUN_ROWS + row, BLOCK // LANES)
+            for plane, piece in enumerate((cell_sorted, weight_sorted, innov_sorted)):
+                at = plane * RUN_ROWS + row
+                send_out[index, at : at + 1, :] = piece[
+                    line : line + 1, LANES * half : LANES * (half + 1)
+                ]
+        send_out[index, 4 * RUN_ROWS : SEND_ROWS, :] = jnp.broadcast_to(
+            longest, (SEND_ROWS - 4 * RUN_ROWS, LANES)
+        )
+    lane_index, row_index = look_up_indices(rows)
 
     def one_level(index, carry):
-        found = look_up(table_ref, index, run_cells(send_out, index), lane_iota, line_iota)
-        for part in range(RUN_BLOCKS):
-            send_out[index, 3 * RUN_BLOCKS + part : 3 * RUN_BLOCKS + part + 1, :] = found[part]
+        found = look_up(table_ref, index, run_pieces(send_out, index, 0), lane_index, row_index)
+        for row in range(RUN_ROWS):
+            at = 3 * RUN_ROWS + row
+            send_out[index, at : at + 1, :] = found[row]
         return carry
 
-    lax.fori_loop(0, levels, one_level, 0)
+    lax.fori_loop(0, levels, one_level, 0, unroll=UNROLL)
 
 
 def pack_slots(scalars, level, cell, weight, innov, table):
     lines = level.shape[0]
     levels = table.shape[0]
-    places = levels * RUN_BLOCKS
+    places = levels * RUN // BLOCK
     whole = pl.BlockSpec(memory_space=VMEM)
     return pl.pallas_call(
         pack_kernel,
-        out_shape=jax.ShapeDtypeStruct((levels, SEND_ROWS, BLOCK), F32),
+        out_shape=jax.ShapeDtypeStruct((levels, SEND_ROWS, LANES), F32),
         in_specs=[pl.BlockSpec(memory_space=SMEM)] + [whole] * 5,
         out_specs=whole,
         scratch_shapes=[
@@ -166,7 +196,7 @@
             VMEM((PLANES, lines, LANES), F32),
             VMEM((PLANES * places, BLOCK), F32),
         ],
-        compiler_params=pltpu.CompilerParams(vmem_limit_bytes=24 << 20),
+        compiler_params=pltpu.CompilerParams(vmem_limit_bytes=16 << 20),
         cost_estimate=pl.CostEstimate(flops=25 * 10**9, bytes_accessed=4 << 20, transcendentals=0),
         name="pack_slots",
     )(scalars, level, cell, weight, innov, table)
@@ -174,19 +204,18 @@
 
 def term_kernel(table_ref, run_ref, term_out):
     groups, rows, width = table_ref.shape
-    lane_iota = lax.broadcasted_iota(jnp.int32, (BLOCK, BLOCK), 0)
-    line_iota = lax.broadcasted_iota(jnp.int32, (rows * width // BLOCK, BLOCK), 0)
+    lane_index, row_index = look_up_indices(rows)
 
     def one_group(group, carry):
-        found = look_up(table_ref, group, run_cells(run_ref, group), lane_iota, line_iota)
-        for part in range(RUN_BLOCKS):
-            row = 3 * RUN_BLOCKS + part
-            term_out[pl.ds(group * RUN_BLOCKS + part, 1), :] = (
-                found[part] * run_ref[group, row : row + 1, :]
+        found = look_up(table_ref, group, run_pieces(run_ref, group, 0), lane_index, row_index)
+        for row in range(RUN_ROWS):
+            at = 3 * RUN_ROWS + row
+            term_out[pl.ds(group * RUN_ROWS + row, 1), :] = (
+                found[row] * run_ref[group, at : at + 1, :]
             )
         return carry
 
-    lax.fori_loop(0, groups, one_group, 0)
+    lax.fori_loop(0, groups, one_group, 0, unroll=UNROLL)
 
 
 def slot_terms(table, runs):
@@ -194,10 +223,10 @@
     whole = pl.BlockSpec(memory_space=VMEM)
     return pl.pallas_call(
         term_kernel,
-        out_shape=jax.ShapeDtypeStruct((groups * RUN_BLOCKS, BLOCK), F32),
+        out_shape=jax.ShapeDtypeStruct((groups * RUN_ROWS, LANES), F32),
         in_specs=[whole, whole],
         out_specs=whole,
-        compiler_params=pltpu.CompilerParams(vmem_limit_bytes=24 << 20),
+        compiler_params=pltpu.CompilerParams(vmem_limit_bytes=12 << 20),
         cost_estimate=pl.CostEstimate(flops=4 * 10**9, bytes_accessed=3 << 20, transcendentals=0),
         name="slot_terms",
     )(table, runs)
@@ -206,24 +235,27 @@
 def add_kernel(run_ref, model_ref, field_out):
     groups, rows, width = field_out.shape
     parts = width // BLOCK
-    lane_iota = lax.broadcasted_iota(jnp.int32, (BLOCK, RUN), 0)
-    line_iota = lax.broadcasted_iota(jnp.int32, (rows * parts, RUN), 0)
+    middle = ROW_STRIDE * parts // 2
+    lane_index = small_float(lax.broadcasted_iota(jnp.int32, (BLOCK, RUN), 0))
+    row_index = lax.broadcasted_iota(jnp.int32, (rows, RUN), 0)
+    line_index = jnp.concatenate(
+        [small_float(row_index + (ROW_STRIDE * part - middle)) for part in range(parts)], axis=0
+    )
 
     def one_group(group, carry):
-        def row_of(first):
+        def values_of(first):
             return jnp.concatenate(
-                [run_ref[group, first + part : first + part + 1, :] for part in range(RUN_BLOCKS)],
-                axis=1,
+                [run_ref[group, first + row : first + row + 1, :] for row in range(RUN_ROWS)], axis=1
             )
 
-        cell = row_of(0).astype(jnp.int32)
+        cell = values_of(0).astype(jnp.int32)
         model = jnp.concatenate(
-            [model_ref[pl.ds(group * RUN_BLOCKS + part, 1), :] for part in range(RUN_BLOCKS)], axis=1
-        )
-        weighted = row_of(RUN_BLOCKS) * (model - row_of(2 * RUN_BLOCKS))
-        value = row_of(3 * RUN_BLOCKS) * weighted
-        lines = jnp.where(line_iota == (cell >> 8), value, 0.0).astype(BF16)
-        chosen = jnp.where(lane_iota == (cell & (BLOCK - 1)), 1.0, 0.0).astype(BF16)
+            [model_ref[pl.ds(group * RUN_ROWS + row, 1), :] for row in range(RUN_ROWS)], axis=1
+        )
+        weighted = values_of(RUN_ROWS) * (model - values_of(2 * RUN_ROWS))
+        value = (values_of(3 * RUN_ROWS) * weighted).astype(BF16)
+        lines = jnp.where(line_index == small_float((cell >> 8) - middle), value, jnp.zeros((), BF16))
+        chosen = jnp.where(lane_index == small_float(cell & (BLOCK - 1)), jnp.ones((), BF16), jnp.zeros((), BF16))
         total = lax.dot_general(
             lines, chosen, (((1,), (1,)), ((), ())), preferred_element_type=F32
         )
@@ -233,7 +265,7 @@
             ].astype(field_out.dtype)
         return carry
 
-    lax.fori_loop(0, groups, one_group, 0)
+    lax.fori_loop(0, groups, one_group, 0, unroll=UNROLL)
 
 
 def add_slots(runs, model, rows, width, dtype):
@@ -244,7 +276,7 @@
         out_shape=jax.ShapeDtypeStruct((groups, rows, width), dtype),
         in_specs=[whole, whole],
         out_specs=whole,
-        compiler_params=pltpu.CompilerParams(vmem_limit_bytes=24 << 20),
+        compiler_params=pltpu.CompilerParams(vmem_limit_bytes=16 << 20),
         cost_estimate=pl.CostEstimate(flops=4 * 10**9, bytes_accessed=3 << 20, transcendentals=0),
         name="add_slots",
     )(runs, model)
@@ -288,11 +320,11 @@
     width = round_up(columns, BLOCK)
     padding = ((0, 0), (0, pad_rows - rows), (0, width - columns))
 
-    alpha_slab = exchange(alpha[0])
+    alpha_slab = exchange(jnp.pad(alpha[0], padding))
 
     as_lines = lambda value: value.reshape(slots // LANES, LANES)
     column = as_lines(obs_col)
-    cell = ((column >> 8) * pad_rows + as_lines(obs_row)) * BLOCK + (column & (BLOCK - 1))
+    cell = ((column >> 8) * ROW_STRIDE + as_lines(obs_row)) * BLOCK + (column & (BLOCK - 1))
     pert_table = jnp.pad(perturbation[0], padding)
 
     def packed_chunk(chunk):
@@ -329,28 +361,24 @@
     )
     lon_root, lat_root = lax.optimization_barrier((lon_root, lat_root))
 
-    padded = jnp.pad(alpha_slab, padding).reshape(tiles * pad_rows, width)
+    padded = alpha_slab.reshape(tiles * pad_rows, width)
     spread = localize(padded, lat_root, lon_root).astype(BF16).reshape(tiles, pad_rows, width)
 
     def chunk_field(chunk_run, dtype):
         model = sum_members(slot_terms(spread, chunk_run))
         return add_slots(chunk_run, model, pad_rows, width, dtype)
 
-    def one_run():
-        return chunk_field(runs, BF16)
-
-    def many_runs():
+    def many_runs(_):
         def one_chunk(chunk, field):
             return field + chunk_field(exchange(packed_chunk(chunk)), F32)
 
         start = jnp.zeros((tiles, pad_rows, width), F32)
         return lax.fori_loop(0, (longest + RUN - 1) // RUN, one_chunk, start).astype(BF16)
 
-    sensitive = lax.cond(longest > RUN, many_runs, one_run)
+    sensitive = lax.cond(longest > RUN, many_runs, lambda field: field, chunk_field(runs, BF16))
     back = localize(sensitive.reshape(tiles * pad_rows, width), lat_root, lon_root)
-    back = back.reshape(tiles, pad_rows, width)[:, :rows, :columns]
-    gradient = (alpha_slab.astype(F32) + back).astype(BF16)
-    return exchange(gradient)[None]
+    gradient = (padded.astype(F32) + back).astype(BF16)
+    return exchange(gradient.reshape(tiles, pad_rows, width))[None, :, :rows, :columns]
 
 
 def solution(mesh):

time: 201 us -> 188 us (0.935)
  Pallas kernels: 44.6 us -> 37.1 us
  other arithmetic: 13.4 us -> 10 us
  waiting for transfers between devices: 21.2 us -> 23.6 us
  local copies, waits for them, and re-layouts: 15.8 us -> 13.4 us
    all_to_all x2, waiting for transfers between devices: 11 us -> 15.1 us  [exchange(): lax.all_to_all(value, 'tile', split_axis=0, concat_axis=0, tiled=True)]
    pallas_call x1, Pallas kernels: 29.2 us -> 26 us  [pack_slots(): pl.pallas_call(pack_kernel, out_shape=jax.ShapeDtypeStruct((levels, SEND_...]
    convert_element_type x1 -> x0, other arithmetic: 3.08 us -> none  [shards(): gradient = (alpha_slab.astype(F32) + back).astype(BF16)]
    unnamed x28 -> x24, local copies, waits for them, and re-layouts: 10 us -> 7.39 us
    pallas_call x1, Pallas kernels: 7.56 us -> 5.32 us  [add_slots(): pl.pallas_call(add_kernel, out_shape=jax.ShapeDtypeStruct((groups, rows,...]
    pallas_call x1, Pallas kernels: 7.82 us -> 5.73 us  [slot_terms(): pl.pallas_call(term_kernel, out_shape=jax.ShapeDtypeStruct((groups * RUN_...]
  transfers between devices with their start and end apart: 6 -> 6, of which waited for: 6 -> 6; matrix products, arithmetic and copies ran while one was open for 12% -> 12% of each run, Pallas kernels for 15% -> 14%
where the time goes in v2:
time: 188 us
  blocking collectives  57.6 us (31%)
  Pallas kernels  37.1 us (20%)
  starting transfers between devices  24.2 us (13%)
  waiting for transfers between devices  23.6 us (13%)
  matrix products  18.6 us (10%)
  local copies, waits for them, and re-layouts  13.4 us (7%)
  other arithmetic  10 us (5%)
  between operations  2.91 us (2%)
    all_to_all x1, blocking collectives, exchange(): lax.all_to_all(value, 'tile', split_axis=0, concat_axis=0, tiled=True)  57.6 us
    pallas_call x1, Pallas kernels, pack_slots(): pl.pallas_call(pack_kernel, out_shape=jax.ShapeDtypeStruct((levels, SEND_...  26 us
    dot_general x2, matrix products, localize(): return jnp.dot(lat_root, zonal, preferred_element_type=F32)  18.6 us
    all_to_all x2, starting transfers between devices, exchange(): lax.all_to_all(value, 'tile', split_axis=0, concat_axis=0, tiled=True)  16.2 us
    all_to_all x2, waiting for transfers between devices, exchange(): lax.all_to_all(value, 'tile', split_axis=0, concat_axis=0, tiled=True)  15.1 us
    convert_element_type x2, other arithmetic, square_root(): return values.astype(BF16)  9.06 us
    ppermute x4, waiting for transfers between devices, sum_members(): lax.ppermute(value, 'mem', [(i, i ^ step) for i in range(members)])  8.5 us
    ppermute x4, starting transfers between devices, sum_members(): lax.ppermute(value, 'mem', [(i, i ^ step) for i in range(members)])  8.04 us
  transfers between devices with their start and end apart: 6, of which 6 were waited for; matrix products, arithmetic and copies ran while one was open for 12% of the time, Pallas kernels for 14%

profile of v2, /device:TPU:32, one launch (start us, length us, event | category | flops | bytes accessed | tf_op | source)
XLA Modules:
  0.0 187.5 jit_solution(10305228228774043690)
XLA Ops:
  0.0 2.8 %copy.20 = bf16[1,16,45,1440]{3,2,1,0:T(8,128)(2,1)S(1)} copy(bf16[1,16,45,1440]{3,1,2,0:T(8,128)(2,1)} %param.14) | data formatting | bytes 4147200 | tf_op args[0]
  2.8 1.7 pad.7
  4.5 9.6 %all-to-all-start.1 = ((bf16[16,48,1536]{2,1,0:T(8,128)(2,1)}), bf16[16,48,1536]{2,1,0:T(8,128)(2,1)S(1)}, u32[]{:S(2)}, u32[]{:S(2)}) async-start(bf16[16,48,1536]{2,1,0:T(8,128)(2,1)} %pad.7), calls=%async_computation.1 | async-start | bytes 4718592 | tf_op jit(solution)/shard_map/all_to_all | solution.py:300
  17.7 2.8 %copy.19 = bf16[1,16,45,1440]{3,2,1,0:T(8,128)(2,1)S(1)} copy(bf16[1,16,45,1440]{3,1,2,0:T(8,128)(2,1)} %param.15) | data formatting | bytes 4147200 | tf_op args[1]
  20.8 2.6 %select_convert_fusion = bf16[768,768]{1,0:T(8,128)(2,1)} fusion(f32[]{:T(128)S(6)} %sqrt.7, f32[]{:T(128)} %bitcast.14, f32[768]{0:T(1024)S(1)} %fusion.10, pred[768]{0:T(1024)(128)(4,1)S(1)} %fusion.14), kind=kLoop, calls=%fused_computation.17 | loop fusion | flops 5898240 | bytes 1183496 | tf_op jit(solution)/shard_map/convert_element_type | solution.py:36
  23.5 6.4 %fusion.7 = bf16[1536,1536]{1,0:T(8,128)(2,1)} fusion(f32[]{:T(128)S(6)} %sqrt.6, f32[]{:T(128)} %bitcast.13, f32[1536]{0:T(1024)S(1)} %iota_convert_fusion, pred[1536]{0:T(1024)(128)(4,1)S(1)} %iota_compare_fusion), kind=kLoop, calls=%fused_computation.9 | loop fusion | flops 28311552 | bytes 4726280 | tf_op jit(solution)/shard_map/convert_element_type | solution.py:36
  30.2 26.0 %pack_slots.2 = f32[16,40,128]{2,1,0:T(8,128)} custom-call(s32[2]{0:T(128)S(1)} %pad_add_fusion.1.scalar_ref, s32[128,128]{1,0:T(8,128)S(1)} %bitcast.44, s32[128,128]{1,0:T(8,128)S(1)} %bitcast.42, f32[128,128]{1,0:T(8,128)S(1)} %bitcast.46, f32[128,128]{1,0:T(8,128)S(1)} %bitcast.48, bf16[16,48,1536]{2,1,0:T(8,128)(2,1)S(1)} %pad.8.table_ref), custom_call_target="tpu_custom_call" | custom-call | flops 24999999488 | bytes 4194304 | tf_op jit(solution)/shard_map/pack_slots/pallas_call | solution.py:189
  56.2 12.5 %all-to-all-done.1 = bf16[16,48,1536]{2,1,0:T(8,128)(2,1)S(1)} async-done(((bf16[16,48,1536]{2,1,0:T(8,128)(2,1)}), bf16[16,48,1536]{2,1,0:T(8,128)(2,1)S(1)}, u32[]{:S(2)}, u32[]{:S(2)}) %all-to-all-start.1) | async-done | bytes 2359328 | tf_op jit(solution)/shard_map/all_to_all | solution.py:300
  68.7 6.6 %all-to-all-start.2 = ((f32[16,40,128]{2,1,0:T(8,128)}), f32[16,40,128]{2,1,0:T(8,128)S(1)}, u32[]{:S(2)}, u32[]{:S(2)}) async-start(f32[16,40,128]{2,1,0:T(8,128)} %pack_slots.2), calls=%async_computation.2 | async-start | bytes 655360 | tf_op jit(solution)/shard_map/all_to_all | solution.py:300
  75.3 8.9 %convolution_convert_fusion.1 = bf16[768,1536]{1,0:T(8,128)(2,1)} fusion(bf16[768,768]{1,0:T(8,128)(2,1)} %select_convert_fusion, bf16[768,1536]{1,0:T(8,128)(2,1)S(1)} %bitcast.39, bf16[1536,1536]{1,0:T(8,128)(2,1)} %fusion.7), kind=kOutput, calls=%fused_computation.12 | convolution fusion | flops 5438177280 | bytes 10616832 | tf_op jit(solution)/shard_map/dot_general | solution.py:287
  84.1 2.6 %all-to-all-done.2.run_ref = f32[16,40,128]{2,1,0:T(8,128)S(1)} async-done(((f32[16,40,128]{2,1,0:T(8,128)}), f32[16,40,128]{2,1,0:T(8,128)S(1)}, u32[]{:S(2)}, u32[]{:S(2)}) %all-to-all-start.2) | async-done | bytes 327712 | tf_op jit(solution)/shard_map/all_to_all | solution.py:300
  86.8 5.7 %slot_terms.2 = f32[144,128]{1,0:T(8,128)S(1)} custom-call(bf16[16,48,1536]{2,1,0:T(8,128)(2,1)} %bitcast.50, f32[16,40,128]{2,1,0:T(8,128)S(1)} %all-to-all-done.2.run_ref), custom_call_target="tpu_custom_call" | custom-call | flops 4000000000 | bytes 3145728 | tf_op jit(solution)/shard_map/slot_terms/pallas_call | solution.py:224
  92.8 1.3 collective-permute-done.4
  94.0 1.7 collective-permute-start.5
  95.7 2.8 %collective-permute-done.5 = f32[144,128]{1,0:T(8,128)S(1)} collective-permute-done((f32[144,128]{1,0:T(8,128)S(1)}, f32[144,128]{1,0:T(8,128)S(1)}, u32[]{:S(2)}, u32[]{:S(2)}) %collective-permute-start.5) | collective-permute-done | bytes 73760 | tf_op jit(solution)/shard_map/ppermute | solution.py:294
  98.5 3.3 %collective-permute-start.6 = (f32[144,128]{1,0:T(8,128)S(1)}, f32[144,128]{1,0:T(8,128)S(1)}, u32[]{:S(2)}, u32[]{:S(2)}) collective-permute-start(f32[144,128]{1,0:T(8,128)S(1)} %add.102), channel_id=1, source_target_pairs={{0,64},{16,80},{32,96},{48,112},{64,0},{80,16},{96,32},{112,48},{1... | collective-permute-start | bytes 221192 | tf_op jit(solution)/shard_map/ppermute | solution.py:294
  101.8 2.7 %collective-permute-done.6 = f32[144,128]{1,0:T(8,128)S(1)} collective-permute-done((f32[144,128]{1,0:T(8,128)S(1)}, f32[144,128]{1,0:T(8,128)S(1)}, u32[]{:S(2)}, u32[]{:S(2)}) %collective-permute-start.6) | collective-permute-done | bytes 73760 | tf_op jit(solution)/shard_map/ppermute | solution.py:294
  104.5 2.8 %collective-permute-start.7 = (f32[144,128]{1,0:T(8,128)S(1)}, f32[144,128]{1,0:T(8,128)S(1)}, u32[]{:S(2)}, u32[]{:S(2)}) collective-permute-start(f32[144,128]{1,0:T(8,128)S(1)} %add.103), channel_id=1, source_target_pairs={{0,128},{16,144},{32,160},{48,176},{64,192},{80,208},{96,224},{112... | collective-permute-start | bytes 221192 | tf_op jit(solution)/shard_map/ppermute | solution.py:294
  108.6 1.8 collective-permute-done.7
  110.4 5.3 %add_slots.2 = bf16[16,48,1536]{2,1,0:T(8,128)(2,1)} custom-call(f32[16,40,128]{2,1,0:T(8,128)S(1)} %all-to-all-done.2.run_ref, f32[144,128]{1,0:T(8,128)S(1)} %add.104.model_ref), custom_call_target="tpu_custom_call" | custom-call | flops 4000000000 | bytes 3145728 | tf_op jit(solution)/shard_map/add_slots/pallas_call | solution.py:274
  115.7 1.7 copy-done.1
  117.4 9.7 %add_convert_fusion = bf16[768,1536]{1,0:T(8,128)(2,1)} fusion(bf16[768,1536]{1,0:T(8,128)(2,1)S(1)} %bitcast.40, bf16[768,768]{1,0:T(8,128)(2,1)} %select_convert_fusion, bf16[768,1536]{1,0:T(8,128)(2,1)} %get-tuple-element.100, bf16[1536,1536]{1,0:T(8,128)(2,1)} %fusion.7), kind=kOutput, calls=%fused_computation.10 | convolution fusion | flops 5440536576 | bytes 12976128 | tf_op jit(solution)/shard_map/dot_general | solution.py:287
  127.1 57.6 %all_to_all.21 = bf16[16,48,1536]{2,1,0:T(8,128)(2,1)S(1)} all-to-all(bf16[16,48,1536]{2,1,0:T(8,128)(2,1)} %bitcast.41), channel_id=1, replica_groups=mesh['mem'=16,'tile'=16] {'tile'}, dimensions={0} | all-to-all | bytes 4718592 | tf_op jit(solution)/shard_map/all_to_all | solution.py:300
  184.9 2.6 %copy.16 = bf16[1,16,45,1440]{3,1,2,0:T(8,128)(2,1)} copy(bf16[1,16,45,1440]{3,2,1,0:T(8,128)(2,1)S(1)} %slice_bitcast_fusion) | data formatting | bytes 4147200 | tf_op jit(solution)/shard_map/broadcast_in_dim | solution.py:381
  (38 shorter events, 3.0 us)
Async XLA Ops:
  4.5 10.4 %copy-start.13 = (f32[16]{0:T(128)S(1)}, f32[16]{0:T(128)}, u32[]{:S(2)}) copy-start(f32[16]{0:T(128)} %param.17) | copy-start | bytes 196
  4.5 11.8 %copy-start.14 = (f32[16]{0:T(128)S(1)}, f32[16]{0:T(128)}, u32[]{:S(2)}) copy-start(f32[16]{0:T(128)} %param.16) | copy-start | bytes 196
  4.5 64.2 %all-to-all-start.1 = ((bf16[16,48,1536]{2,1,0:T(8,128)(2,1)}), bf16[16,48,1536]{2,1,0:T(8,128)(2,1)S(1)}, u32[]{:S(2)}, u32[]{:S(2)}) async-start(bf16[16,48,1536]{2,1,0:T(8,128)(2,1)} %pad.7), calls=%async_computation.1 | async-start | bytes 4718592 | tf_op jit(solution)/shard_map/all_to_all | solution.py:300
  20.8 9.3 %copy-start.2 = (bf16[16,48,1536]{2,1,0:T(8,128)(2,1)}, bf16[16,48,1536]{2,1,0:T(8,128)(2,1)S(1)}, u32[]{:S(2)}) copy-start(bf16[16,48,1536]{2,1,0:T(8,128)(2,1)S(1)} %pad.8.table_ref) | copy-start | bytes 7077892
  23.5 6.5 %copy-start.3 = (s32[1,16384]{1,0:T(1,128)S(1)}, s32[1,16384]{1,0:T(1,128)}, u32[]{:S(2)}) copy-start(s32[1,16384]{1,0:T(1,128)} %param.20) | copy-start | bytes 196612
  23.5 6.5 %copy-start.4 = (s32[1,16384]{1,0:T(1,128)S(1)}, s32[1,16384]{1,0:T(1,128)}, u32[]{:S(2)}) copy-start(s32[1,16384]{1,0:T(1,128)} %param.19) | copy-start | bytes 196612
  23.5 6.7 %copy-start.7 = (s32[1,16384]{1,0:T(1,128)S(1)}, s32[1,16384]{1,0:T(1,128)}, u32[]{:S(2)}) copy-start(s32[1,16384]{1,0:T(1,128)} %param.18) | copy-start | bytes 196612
  23.5 6.7 %copy-start.9 = (f32[1,16384]{1,0:T(1,128)S(1)}, f32[1,16384]{1,0:T(1,128)}, u32[]{:S(2)}) copy-start(f32[1,16384]{1,0:T(1,128)} %param.23) | copy-start | bytes 196612
  23.5 6.7 %copy-start.11 = (f32[1,16384]{1,0:T(1,128)S(1)}, f32[1,16384]{1,0:T(1,128)}, u32[]{:S(2)}) copy-start(f32[1,16384]{1,0:T(1,128)} %param.22) | copy-start | bytes 196612
  30.1 26.1 %copy-start.5 = (s32[1,16384]{1,0:T(1,128)}, s32[1,16384]{1,0:T(1,128)S(1)}, u32[]{:S(2)}) copy-start(s32[1,16384]{1,0:T(1,128)S(1)} %and_add_fusion) | copy-start | bytes 196612
  68.7 15.4 %copy-start = (bf16[16,48,1536]{2,1,0:T(8,128)(2,1)}, bf16[16,48,1536]{2,1,0:T(8,128)(2,1)S(1)}, u32[]{:S(2)}) copy-start(bf16[16,48,1536]{2,1,0:T(8,128)(2,1)S(1)} %all-to-all-done.1) | copy-start | bytes 7077892
  68.7 18.1 %all-to-all-start.2 = ((f32[16,40,128]{2,1,0:T(8,128)}), f32[16,40,128]{2,1,0:T(8,128)S(1)}, u32[]{:S(2)}, u32[]{:S(2)}) async-start(f32[16,40,128]{2,1,0:T(8,128)} %pack_slots.2), calls=%async_computation.2 | async-start | bytes 655360 | tf_op jit(solution)/shard_map/all_to_all | solution.py:300
  92.5 1.5 collective-permute-start.4
  94.0 4.4 %collective-permute-start.5 = (f32[144,128]{1,0:T(8,128)S(1)}, f32[144,128]{1,0:T(8,128)S(1)}, u32[]{:S(2)}, u32[]{:S(2)}) collective-permute-start(f32[144,128]{1,0:T(8,128)S(1)} %add.101), channel_id=1, source_target_pairs={{0,32},{16,48},{32,0},{48,16},{64,96},{80,112},{96,64},{112,80},{1... | collective-permute-start | bytes 221192 | tf_op jit(solution)/shard_map/ppermute | solution.py:294
  98.5 5.9 %collective-permute-start.6 = (f32[144,128]{1,0:T(8,128)S(1)}, f32[144,128]{1,0:T(8,128)S(1)}, u32[]{:S(2)}, u32[]{:S(2)}) collective-permute-start(f32[144,128]{1,0:T(8,128)S(1)} %add.102), channel_id=1, source_target_pairs={{0,64},{16,80},{32,96},{48,112},{64,0},{80,16},{96,32},{112,48},{1... | collective-permute-start | bytes 221192 | tf_op jit(solution)/shard_map/ppermute | solution.py:294
  104.5 5.9 %collective-permute-start.7 = (f32[144,128]{1,0:T(8,128)S(1)}, f32[144,128]{1,0:T(8,128)S(1)}, u32[]{:S(2)}, u32[]{:S(2)}) collective-permute-start(f32[144,128]{1,0:T(8,128)S(1)} %add.103), channel_id=1, source_target_pairs={{0,128},{16,144},{32,160},{48,176},{64,192},{80,208},{96,224},{112... | collective-permute-start | bytes 221192 | tf_op jit(solution)/shard_map/ppermute | solution.py:294
  115.7 1.7 copy-start.1

commit v3 on v2

--- a/solution.py
+++ b/solution.py
@@ -368,17 +368,21 @@
         model = sum_members(slot_terms(spread, chunk_run))
         return add_slots(chunk_run, model, pad_rows, width, dtype)
 
+    def gradient_of(field):
+        back = localize(field.reshape(tiles * pad_rows, width), lat_root, lon_root)
+        return (padded.astype(F32) + back).astype(BF16).reshape(tiles, pad_rows, width)
+
     def many_runs(_):
         def one_chunk(chunk, field):
             return field + chunk_field(exchange(packed_chunk(chunk)), F32)
 
         start = jnp.zeros((tiles, pad_rows, width), F32)
-        return lax.fori_loop(0, (longest + RUN - 1) // RUN, one_chunk, start).astype(BF16)
-
-    sensitive = lax.cond(longest > RUN, many_runs, lambda field: field, chunk_field(runs, BF16))
-    back = localize(sensitive.reshape(tiles * pad_rows, width), lat_root, lon_root)
-    gradient = (padded.astype(F32) + back).astype(BF16)
-    return exchange(gradient.reshape(tiles, pad_rows, width))[None, :, :rows, :columns]
+        chunks = (longest + RUN - 1) // RUN
+        return gradient_of(lax.fori_loop(0, chunks, one_chunk, start).astype(BF16))
+
+    first = lax.optimization_barrier(gradient_of(chunk_field(runs, BF16)))
+    gradient = lax.cond(longest > RUN, many_runs, lambda done: done, first)
+    return exchange(gradient)[None, :, :rows, :columns]
 
 
 def solution(mesh):

time: 188 us -> 185 us (0.984)
    unnamed x24 -> x22, local copies, waits for them, and re-layouts: 7.39 us -> 5.72 us
  transfers between devices with their start and end apart: 6 -> 6, of which waited for: 6 -> 6; matrix products, arithmetic and copies ran while one was open for 12% -> 13% of each run, Pallas kernels for 14% -> 14%
where the time goes in v3:
time: 185 us; the launch traced here: 184 us
  blocking collectives  57.6 us (31%)
  Pallas kernels  35.7 us (19%)
  starting transfers between devices  24.2 us (13%)
  waiting for transfers between devices  24 us (13%)
  matrix products  18.2 us (10%)
  local copies, waits for them, and re-layouts  11.7 us (6%)
  other arithmetic  9.87 us (5%)
  between operations  2.78 us (2%)
    all_to_all x1, blocking collectives, exchange(): lax.all_to_all(value, 'tile', split_axis=0, concat_axis=0, tiled=True)  57.6 us
    pallas_call x1, Pallas kernels, pack_slots(): pl.pallas_call(pack_kernel, out_shape=jax.ShapeDtypeStruct((levels, SEND_...  26 us
    dot_general x2, matrix products, localize(): return jnp.dot(lat_root, zonal, preferred_element_type=F32)  18.2 us
    all_to_all x2, starting transfers between devices, exchange(): lax.all_to_all(value, 'tile', split_axis=0, concat_axis=0, tiled=True)  16.2 us
    all_to_all x2, waiting for transfers between devices, exchange(): lax.all_to_all(value, 'tile', split_axis=0, concat_axis=0, tiled=True)  15.5 us
    convert_element_type x2, other arithmetic, square_root(): return values.astype(BF16)  8.93 us
    ppermute x4, waiting for transfers between devices, sum_members(): lax.ppermute(value, 'mem', [(i, i ^ step) for i in range(members)])  8.52 us
    ppermute x4, starting transfers between devices, sum_members(): lax.ppermute(value, 'mem', [(i, i ^ step) for i in range(members)])  8.03 us
  transfers between devices with their start and end apart: 6, of which 6 were waited for; matrix products, arithmetic and copies ran while one was open for 13% of the time, Pallas kernels for 14%

profile of v3, /device:TPU:32, one launch (start us, length us, event | category | flops | bytes accessed | tf_op | source)
XLA Modules:
  0.0 184.0 jit_solution(3917913541510983108)
XLA Ops:
  0.0 2.8 %copy.20 = bf16[1,16,45,1440]{3,2,1,0:T(8,128)(2,1)S(1)} copy(bf16[1,16,45,1440]{3,1,2,0:T(8,128)(2,1)} %param.14) | data formatting | bytes 4147200 | tf_op args[0]
  2.8 1.7 pad.7
  4.5 9.6 %all-to-all-start.1 = ((bf16[16,48,1536]{2,1,0:T(8,128)(2,1)}), bf16[16,48,1536]{2,1,0:T(8,128)(2,1)S(1)}, u32[]{:S(2)}, u32[]{:S(2)}) async-start(bf16[16,48,1536]{2,1,0:T(8,128)(2,1)} %pad.7), calls=%async_computation.1 | async-start | bytes 4718592 | tf_op jit(solution)/shard_map/all_to_all | solution.py:300
  17.5 2.8 %copy.19 = bf16[1,16,45,1440]{3,2,1,0:T(8,128)(2,1)S(1)} copy(bf16[1,16,45,1440]{3,1,2,0:T(8,128)(2,1)} %param.15) | data formatting | bytes 4147200 | tf_op args[1]
  20.6 2.5 %select_convert_fusion = bf16[768,768]{1,0:T(8,128)(2,1)} fusion(f32[]{:T(128)S(6)} %sqrt.7, f32[]{:T(128)} %bitcast.15, f32[768]{0:T(1024)S(1)} %fusion.11, pred[768]{0:T(1024)(128)(4,1)S(1)} %fusion.15), kind=kLoop, calls=%fused_computation.20 | loop fusion | flops 5898240 | bytes 1183496 | tf_op jit(solution)/shard_map/convert_element_type | solution.py:36
  23.1 6.4 %fusion.8 = bf16[1536,1536]{1,0:T(8,128)(2,1)} fusion(f32[]{:T(128)S(6)} %sqrt.6, f32[]{:T(128)} %bitcast.14, f32[1536]{0:T(1024)S(1)} %iota_convert_fusion, pred[1536]{0:T(1024)(128)(4,1)S(1)} %iota_compare_fusion), kind=kLoop, calls=%fused_computation.12 | loop fusion | flops 28311552 | bytes 4726280 | tf_op jit(solution)/shard_map/convert_element_type | solution.py:36
  29.8 26.0 %pack_slots.2 = f32[16,40,128]{2,1,0:T(8,128)} custom-call(s32[2]{0:T(128)S(1)} %pad_add_fusion.1.scalar_ref, s32[128,128]{1,0:T(8,128)S(1)} %bitcast.56, s32[128,128]{1,0:T(8,128)S(1)} %bitcast.54, f32[128,128]{1,0:T(8,128)S(1)} %bitcast.58, f32[128,128]{1,0:T(8,128)S(1)} %bitcast.60, bf16[16,48,1536]{2,1,0:T(8,128)(2,1)S(1)} %pad.8.table_ref), custom_call_target="tpu_custom_call" | custom-call | flops 24999999488 | bytes 4194304 | tf_op jit(solution)/shard_map/pack_slots/pallas_call | solution.py:189
  55.8 12.9 %all-to-all-done.1 = bf16[16,48,1536]{2,1,0:T(8,128)(2,1)S(1)} async-done(((bf16[16,48,1536]{2,1,0:T(8,128)(2,1)}), bf16[16,48,1536]{2,1,0:T(8,128)(2,1)S(1)}, u32[]{:S(2)}, u32[]{:S(2)}) %all-to-all-start.1) | async-done | bytes 2359328 | tf_op jit(solution)/shard_map/all_to_all | solution.py:300
  68.7 6.6 %all-to-all-start.2 = ((f32[16,40,128]{2,1,0:T(8,128)}), f32[16,40,128]{2,1,0:T(8,128)S(1)}, u32[]{:S(2)}, u32[]{:S(2)}) async-start(f32[16,40,128]{2,1,0:T(8,128)} %pack_slots.2), calls=%async_computation.2 | async-start | bytes 655360 | tf_op jit(solution)/shard_map/all_to_all | solution.py:300
  75.3 8.9 %convolution_convert_fusion.2 = bf16[768,1536]{1,0:T(8,128)(2,1)} fusion(bf16[768,768]{1,0:T(8,128)(2,1)} %select_convert_fusion, bf16[768,1536]{1,0:T(8,128)(2,1)S(1)} %bitcast.49, bf16[1536,1536]{1,0:T(8,128)(2,1)} %fusion.8), kind=kOutput, calls=%fused_computation.15 | convolution fusion | flops 5438177280 | bytes 10616832 | tf_op jit(solution)/shard_map/dot_general | solution.py:287
  84.1 2.6 %all-to-all-done.2.run_ref = f32[16,40,128]{2,1,0:T(8,128)S(1)} async-done(((f32[16,40,128]{2,1,0:T(8,128)}), f32[16,40,128]{2,1,0:T(8,128)S(1)}, u32[]{:S(2)}, u32[]{:S(2)}) %all-to-all-start.2) | async-done | bytes 327712 | tf_op jit(solution)/shard_map/all_to_all | solution.py:300
  86.8 5.7 %slot_terms.2 = f32[144,128]{1,0:T(8,128)S(1)} custom-call(bf16[16,48,1536]{2,1,0:T(8,128)(2,1)} %bitcast.62, f32[16,40,128]{2,1,0:T(8,128)S(1)} %all-to-all-done.2.run_ref), custom_call_target="tpu_custom_call" | custom-call | flops 4000000000 | bytes 3145728 | tf_op jit(solution)/shard_map/slot_terms/pallas_call | solution.py:224
  92.8 1.3 collective-permute-done.4
  94.0 1.7 collective-permute-start.5
  95.7 2.8 %collective-permute-done.5 = f32[144,128]{1,0:T(8,128)S(1)} collective-permute-done((f32[144,128]{1,0:T(8,128)S(1)}, f32[144,128]{1,0:T(8,128)S(1)}, u32[]{:S(2)}, u32[]{:S(2)}) %collective-permute-start.5) | collective-permute-done | bytes 73760 | tf_op jit(solution)/shard_map/ppermute | solution.py:294
  98.5 3.3 %collective-permute-start.6 = (f32[144,128]{1,0:T(8,128)S(1)}, f32[144,128]{1,0:T(8,128)S(1)}, u32[]{:S(2)}, u32[]{:S(2)}) collective-permute-start(f32[144,128]{1,0:T(8,128)S(1)} %add.105), channel_id=1, source_target_pairs={{0,64},{16,80},{32,96},{48,112},{64,0},{80,16},{96,32},{112,48},{1... | collective-permute-start | bytes 221192 | tf_op jit(solution)/shard_map/ppermute | solution.py:294
  101.8 2.7 %collective-permute-done.6 = f32[144,128]{1,0:T(8,128)S(1)} collective-permute-done((f32[144,128]{1,0:T(8,128)S(1)}, f32[144,128]{1,0:T(8,128)S(1)}, u32[]{:S(2)}, u32[]{:S(2)}) %collective-permute-start.6) | collective-permute-done | bytes 73760 | tf_op jit(solution)/shard_map/ppermute | solution.py:294
  104.5 2.8 %collective-permute-start.7 = (f32[144,128]{1,0:T(8,128)S(1)}, f32[144,128]{1,0:T(8,128)S(1)}, u32[]{:S(2)}, u32[]{:S(2)}) collective-permute-start(f32[144,128]{1,0:T(8,128)S(1)} %add.106), channel_id=1, source_target_pairs={{0,128},{16,144},{32,160},{48,176},{64,192},{80,208},{96,224},{112... | collective-permute-start | bytes 221192 | tf_op jit(solution)/shard_map/ppermute | solution.py:294
  107.3 0.7 slice_reduce_fusion
  108.6 1.8 collective-permute-done.7
  110.4 3.9 %add_slots.2 = bf16[16,48,1536]{2,1,0:T(8,128)(2,1)S(1)} custom-call(f32[16,40,128]{2,1,0:T(8,128)S(1)} %all-to-all-done.2.run_ref, f32[144,128]{1,0:T(8,128)S(1)} %add.107.model_ref), custom_call_target="tpu_custom_call" | custom-call | flops 4000000000 | bytes 3145728 | tf_op jit(solution)/shard_map/add_slots/pallas_call | solution.py:274
  114.3 9.3 %add_convert_fusion = bf16[768,1536]{1,0:T(8,128)(2,1)} fusion(bf16[768,1536]{1,0:T(8,128)(2,1)} %bitcast.50, bf16[768,768]{1,0:T(8,128)(2,1)} %select_convert_fusion, bf16[768,1536]{1,0:T(8,128)(2,1)S(1)} %bitcast.45, bf16[1536,1536]{1,0:T(8,128)(2,1)} %fusion.8), kind=kOutput, calls=%fused_computation.13 | convolution fusion | flops 5440536576 | bytes 12976128 | tf_op jit(solution)/shard_map/dot_general | solution.py:287
  123.6 57.6 %all_to_all.21 = bf16[16,48,1536]{2,1,0:T(8,128)(2,1)S(1)} all-to-all(bf16[16,48,1536]{2,1,0:T(8,128)(2,1)} %get-tuple-element.218), channel_id=1, replica_groups=mesh['mem'=16,'tile'=16] {'tile'}, dimensions={0} | all-to-all | bytes 4718592 | tf_op jit(solution)/shard_map/all_to_all | solution.py:300
  181.4 2.6 %copy.16 = bf16[1,16,45,1440]{3,1,2,0:T(8,128)(2,1)} copy(bf16[1,16,45,1440]{3,2,1,0:T(8,128)(2,1)S(1)} %slice_bitcast_fusion) | data formatting | bytes 4147200 | tf_op jit(solution)/shard_map/broadcast_in_dim | solution.py:385
  (36 shorter events, 2.2 us)
Async XLA Ops:
  4.5 10.4 %copy-start.14 = (f32[16]{0:T(128)S(1)}, f32[16]{0:T(128)}, u32[]{:S(2)}) copy-start(f32[16]{0:T(128)} %param.17) | copy-start | bytes 196
  4.5 11.5 %copy-start.15 = (f32[16]{0:T(128)S(1)}, f32[16]{0:T(128)}, u32[]{:S(2)}) copy-start(f32[16]{0:T(128)} %param.16) | copy-start | bytes 196
  4.5 64.2 %all-to-all-start.1 = ((bf16[16,48,1536]{2,1,0:T(8,128)(2,1)}), bf16[16,48,1536]{2,1,0:T(8,128)(2,1)S(1)}, u32[]{:S(2)}, u32[]{:S(2)}) async-start(bf16[16,48,1536]{2,1,0:T(8,128)(2,1)} %pad.7), calls=%async_computation.1 | async-start | bytes 4718592 | tf_op jit(solution)/shard_map/all_to_all | solution.py:300
  20.6 9.2 %copy-start.1 = (bf16[16,48,1536]{2,1,0:T(8,128)(2,1)}, bf16[16,48,1536]{2,1,0:T(8,128)(2,1)S(1)}, u32[]{:S(2)}) copy-start(bf16[16,48,1536]{2,1,0:T(8,128)(2,1)S(1)} %pad.8.table_ref) | copy-start | bytes 7077892
  23.1 6.5 %copy-start.4 = (s32[1,16384]{1,0:T(1,128)S(1)}, s32[1,16384]{1,0:T(1,128)}, u32[]{:S(2)}) copy-start(s32[1,16384]{1,0:T(1,128)} %param.20) | copy-start | bytes 196612
  23.1 6.5 %copy-start.5 = (s32[1,16384]{1,0:T(1,128)S(1)}, s32[1,16384]{1,0:T(1,128)}, u32[]{:S(2)}) copy-start(s32[1,16384]{1,0:T(1,128)} %param.19) | copy-start | bytes 196612
  23.1 6.7 %copy-start.8 = (s32[1,16384]{1,0:T(1,128)S(1)}, s32[1,16384]{1,0:T(1,128)}, u32[]{:S(2)}) copy-start(s32[1,16384]{1,0:T(1,128)} %param.18) | copy-start | bytes 196612
  23.1 6.7 %copy-start.10 = (f32[1,16384]{1,0:T(1,128)S(1)}, f32[1,16384]{1,0:T(1,128)}, u32[]{:S(2)}) copy-start(f32[1,16384]{1,0:T(1,128)} %param.23) | copy-start | bytes 196612
  23.1 6.7 %copy-start.12 = (f32[1,16384]{1,0:T(1,128)S(1)}, f32[1,16384]{1,0:T(1,128)}, u32[]{:S(2)}) copy-start(f32[1,16384]{1,0:T(1,128)} %param.22) | copy-start | bytes 196612
  29.8 26.1 %copy-start.6 = (s32[1,16384]{1,0:T(1,128)}, s32[1,16384]{1,0:T(1,128)S(1)}, u32[]{:S(2)}) copy-start(s32[1,16384]{1,0:T(1,128)S(1)} %and_add_fusion) | copy-start | bytes 196612
  68.7 15.4 %copy-start = (bf16[16,48,1536]{2,1,0:T(8,128)(2,1)}, bf16[16,48,1536]{2,1,0:T(8,128)(2,1)S(1)}, u32[]{:S(2)}) copy-start(bf16[16,48,1536]{2,1,0:T(8,128)(2,1)S(1)} %all-to-all-done.1) | copy-start | bytes 7077892
  68.7 18.1 %all-to-all-start.2 = ((f32[16,40,128]{2,1,0:T(8,128)}), f32[16,40,128]{2,1,0:T(8,128)S(1)}, u32[]{:S(2)}, u32[]{:S(2)}) async-start(f32[16,40,128]{2,1,0:T(8,128)} %pack_slots.2), calls=%async_computation.2 | async-start | bytes 655360 | tf_op jit(solution)/shard_map/all_to_all | solution.py:300
  92.5 1.5 collective-permute-start.4
  94.0 4.4 %collective-permute-start.5 = (f32[144,128]{1,0:T(8,128)S(1)}, f32[144,128]{1,0:T(8,128)S(1)}, u32[]{:S(2)}, u32[]{:S(2)}) collective-permute-start(f32[144,128]{1,0:T(8,128)S(1)} %add.104), channel_id=1, source_target_pairs={{0,32},{16,48},{32,0},{48,16},{64,96},{80,112},{96,64},{112,80},{1... | collective-permute-start | bytes 221192 | tf_op jit(solution)/shard_map/ppermute | solution.py:294
  98.5 5.9 %collective-permute-start.6 = (f32[144,128]{1,0:T(8,128)S(1)}, f32[144,128]{1,0:T(8,128)S(1)}, u32[]{:S(2)}, u32[]{:S(2)}) collective-permute-start(f32[144,128]{1,0:T(8,128)S(1)} %add.105), channel_id=1, source_target_pairs={{0,64},{16,80},{32,96},{48,112},{64,0},{80,16},{96,32},{112,48},{1... | collective-permute-start | bytes 221192 | tf_op jit(solution)/shard_map/ppermute | solution.py:294
  104.5 5.9 %collective-permute-start.7 = (f32[144,128]{1,0:T(8,128)S(1)}, f32[144,128]{1,0:T(8,128)S(1)}, u32[]{:S(2)}, u32[]{:S(2)}) collective-permute-start(f32[144,128]{1,0:T(8,128)S(1)} %add.106), channel_id=1, source_target_pairs={{0,128},{16,144},{32,160},{48,176},{64,192},{80,208},{96,224},{112... | collective-permute-start | bytes 221192 | tf_op jit(solution)/shard_map/ppermute | solution.py:294

commit v4 on v3

--- a/solution.py
+++ b/solution.py
@@ -15,6 +15,7 @@
 SEND_ROWS = 40
 ROW_STRIDE = 64
 UNROLL = 4
+SLAB_UNROLL = 8
 F32 = jnp.float32
 BF16 = jnp.bfloat16
 VMEM = pltpu.VMEM
@@ -215,7 +216,7 @@
             )
         return carry
 
-    lax.fori_loop(0, groups, one_group, 0, unroll=UNROLL)
+    lax.fori_loop(0, groups, one_group, 0, unroll=SLAB_UNROLL)
 
 
 def slot_terms(table, runs):
@@ -265,7 +266,7 @@
             ].astype(field_out.dtype)
         return carry
 
-    lax.fori_loop(0, groups, one_group, 0, unroll=UNROLL)
+    lax.fori_loop(0, groups, one_group, 0, unroll=SLAB_UNROLL)
 
 
 def add_slots(runs, model, rows, width, dtype):

time: 185 us -> 184 us (level)
  no operation moved by 1% of the time
where the time goes in v4:
time: 184 us; the launch traced here: 183 us
  blocking collectives  57.6 us (31%)
  Pallas kernels  34.9 us (19%)
  starting transfers between devices  24.1 us (13%)
  waiting for transfers between devices  24 us (13%)
  matrix products  18.2 us (10%)
  local copies, waits for them, and re-layouts  11.7 us (6%)
  other arithmetic  9.87 us (5%)
  between operations  2.78 us (2%)
    all_to_all x1, blocking collectives, exchange(): lax.all_to_all(value, 'tile', split_axis=0, concat_axis=0, tiled=True)  57.6 us
    pallas_call x1, Pallas kernels, pack_slots(): pl.pallas_call(pack_kernel, out_shape=jax.ShapeDtypeStruct((levels, SEND_...  26 us
    dot_general x2, matrix products, localize(): return jnp.dot(lat_root, zonal, preferred_element_type=F32)  18.2 us
    all_to_all x2, starting transfers between devices, exchange(): lax.all_to_all(value, 'tile', split_axis=0, concat_axis=0, tiled=True)  16.2 us
    all_to_all x2, waiting for transfers between devices, exchange(): lax.all_to_all(value, 'tile', split_axis=0, concat_axis=0, tiled=True)  15.5 us
    convert_element_type x2, other arithmetic, square_root(): return values.astype(BF16)  8.93 us
    ppermute x4, waiting for transfers between devices, sum_members(): lax.ppermute(value, 'mem', [(i, i ^ step) for i in range(members)])  8.51 us
    ppermute x4, starting transfers between devices, sum_members(): lax.ppermute(value, 'mem', [(i, i ^ step) for i in range(members)])  7.86 us
  transfers between devices with their start and end apart: 6, of which 6 were waited for; matrix products, arithmetic and copies ran while one was open for 13% of the time, Pallas kernels for 14%

profile of v4, /device:TPU:32, one launch (start us, length us, event | category | flops | bytes accessed | tf_op | source)
XLA Modules:
  0.0 183.1 jit_solution(2190920058920610003)
XLA Ops:
  0.0 2.8 %copy.20 = bf16[1,16,45,1440]{3,2,1,0:T(8,128)(2,1)S(1)} copy(bf16[1,16,45,1440]{3,1,2,0:T(8,128)(2,1)} %param.14) | data formatting | bytes 4147200 | tf_op args[0]
  2.8 1.7 pad.7
  4.5 9.6 %all-to-all-start.1 = ((bf16[16,48,1536]{2,1,0:T(8,128)(2,1)}), bf16[16,48,1536]{2,1,0:T(8,128)(2,1)S(1)}, u32[]{:S(2)}, u32[]{:S(2)}) async-start(bf16[16,48,1536]{2,1,0:T(8,128)(2,1)} %pad.7), calls=%async_computation.1 | async-start | bytes 4718592 | tf_op jit(solution)/shard_map/all_to_all | solution.py:301
  17.5 2.8 %copy.19 = bf16[1,16,45,1440]{3,2,1,0:T(8,128)(2,1)S(1)} copy(bf16[1,16,45,1440]{3,1,2,0:T(8,128)(2,1)} %param.15) | data formatting | bytes 4147200 | tf_op args[1]
  20.6 2.5 %select_convert_fusion = bf16[768,768]{1,0:T(8,128)(2,1)} fusion(f32[]{:T(128)S(6)} %sqrt.7, f32[]{:T(128)} %bitcast.15, f32[768]{0:T(1024)S(1)} %fusion.11, pred[768]{0:T(1024)(128)(4,1)S(1)} %fusion.15), kind=kLoop, calls=%fused_computation.20 | loop fusion | flops 5898240 | bytes 1183496 | tf_op jit(solution)/shard_map/convert_element_type | solution.py:37
  23.1 6.4 %fusion.8 = bf16[1536,1536]{1,0:T(8,128)(2,1)} fusion(f32[]{:T(128)S(6)} %sqrt.6, f32[]{:T(128)} %bitcast.14, f32[1536]{0:T(1024)S(1)} %iota_convert_fusion, pred[1536]{0:T(1024)(128)(4,1)S(1)} %iota_compare_fusion), kind=kLoop, calls=%fused_computation.12 | loop fusion | flops 28311552 | bytes 4726280 | tf_op jit(solution)/shard_map/convert_element_type | solution.py:37
  29.8 26.0 %pack_slots.2 = f32[16,40,128]{2,1,0:T(8,128)} custom-call(s32[2]{0:T(128)S(1)} %pad_add_fusion.1.scalar_ref, s32[128,128]{1,0:T(8,128)S(1)} %bitcast.56, s32[128,128]{1,0:T(8,128)S(1)} %bitcast.54, f32[128,128]{1,0:T(8,128)S(1)} %bitcast.58, f32[128,128]{1,0:T(8,128)S(1)} %bitcast.60, bf16[16,48,1536]{2,1,0:T(8,128)(2,1)S(1)} %pad.8.table_ref), custom_call_target="tpu_custom_call" | custom-call | flops 24999999488 | bytes 4194304 | tf_op jit(solution)/shard_map/pack_slots/pallas_call | solution.py:190
  55.8 12.9 %all-to-all-done.1 = bf16[16,48,1536]{2,1,0:T(8,128)(2,1)S(1)} async-done(((bf16[16,48,1536]{2,1,0:T(8,128)(2,1)}), bf16[16,48,1536]{2,1,0:T(8,128)(2,1)S(1)}, u32[]{:S(2)}, u32[]{:S(2)}) %all-to-all-start.1) | async-done | bytes 2359328 | tf_op jit(solution)/shard_map/all_to_all | solution.py:301
  68.7 6.6 %all-to-all-start.2 = ((f32[16,40,128]{2,1,0:T(8,128)}), f32[16,40,128]{2,1,0:T(8,128)S(1)}, u32[]{:S(2)}, u32[]{:S(2)}) async-start(f32[16,40,128]{2,1,0:T(8,128)} %pack_slots.2), calls=%async_computation.2 | async-start | bytes 655360 | tf_op jit(solution)/shard_map/all_to_all | solution.py:301
  75.3 8.9 %convolution_convert_fusion.2 = bf16[768,1536]{1,0:T(8,128)(2,1)} fusion(bf16[768,768]{1,0:T(8,128)(2,1)} %select_convert_fusion, bf16[768,1536]{1,0:T(8,128)(2,1)S(1)} %bitcast.49, bf16[1536,1536]{1,0:T(8,128)(2,1)} %fusion.8), kind=kOutput, calls=%fused_computation.15 | convolution fusion | flops 5438177280 | bytes 10616832 | tf_op jit(solution)/shard_map/dot_general | solution.py:288
  84.1 2.6 %all-to-all-done.2.run_ref = f32[16,40,128]{2,1,0:T(8,128)S(1)} async-done(((f32[16,40,128]{2,1,0:T(8,128)}), f32[16,40,128]{2,1,0:T(8,128)S(1)}, u32[]{:S(2)}, u32[]{:S(2)}) %all-to-all-start.2) | async-done | bytes 327712 | tf_op jit(solution)/shard_map/all_to_all | solution.py:301
  86.8 5.4 %slot_terms.2 = f32[144,128]{1,0:T(8,128)S(1)} custom-call(bf16[16,48,1536]{2,1,0:T(8,128)(2,1)} %bitcast.62, f32[16,40,128]{2,1,0:T(8,128)S(1)} %all-to-all-done.2.run_ref), custom_call_target="tpu_custom_call" | custom-call | flops 4000000000 | bytes 3145728 | tf_op jit(solution)/shard_map/slot_terms/pallas_call | solution.py:225
  92.2 1.3 collective-permute-done.4
  93.5 1.7 collective-permute-start.5
  95.2 2.8 %collective-permute-done.5 = f32[144,128]{1,0:T(8,128)S(1)} collective-permute-done((f32[144,128]{1,0:T(8,128)S(1)}, f32[144,128]{1,0:T(8,128)S(1)}, u32[]{:S(2)}, u32[]{:S(2)}) %collective-permute-start.5) | collective-permute-done | bytes 73760 | tf_op jit(solution)/shard_map/ppermute | solution.py:295
  98.0 3.3 %collective-permute-start.6 = (f32[144,128]{1,0:T(8,128)S(1)}, f32[144,128]{1,0:T(8,128)S(1)}, u32[]{:S(2)}, u32[]{:S(2)}) collective-permute-start(f32[144,128]{1,0:T(8,128)S(1)} %add.105), channel_id=1, source_target_pairs={{0,64},{16,80},{32,96},{48,112},{64,0},{80,16},{96,32},{112,48},{1... | collective-permute-start | bytes 221192 | tf_op jit(solution)/shard_map/ppermute | solution.py:295
  101.2 2.7 %collective-permute-done.6 = f32[144,128]{1,0:T(8,128)S(1)} collective-permute-done((f32[144,128]{1,0:T(8,128)S(1)}, f32[144,128]{1,0:T(8,128)S(1)}, u32[]{:S(2)}, u32[]{:S(2)}) %collective-permute-start.6) | collective-permute-done | bytes 73760 | tf_op jit(solution)/shard_map/ppermute | solution.py:295
  103.9 2.8 %collective-permute-start.7 = (f32[144,128]{1,0:T(8,128)S(1)}, f32[144,128]{1,0:T(8,128)S(1)}, u32[]{:S(2)}, u32[]{:S(2)}) collective-permute-start(f32[144,128]{1,0:T(8,128)S(1)} %add.106), channel_id=1, source_target_pairs={{0,128},{16,144},{32,160},{48,176},{64,192},{80,208},{96,224},{112... | collective-permute-start | bytes 221192 | tf_op jit(solution)/shard_map/ppermute | solution.py:295
  106.7 0.7 slice_reduce_fusion
  108.0 1.8 collective-permute-done.7
  109.9 3.5 %add_slots.2 = bf16[16,48,1536]{2,1,0:T(8,128)(2,1)S(1)} custom-call(f32[16,40,128]{2,1,0:T(8,128)S(1)} %all-to-all-done.2.run_ref, f32[144,128]{1,0:T(8,128)S(1)} %add.107.model_ref), custom_call_target="tpu_custom_call" | custom-call | flops 4000000000 | bytes 3145728 | tf_op jit(solution)/shard_map/add_slots/pallas_call | solution.py:275
  113.4 9.3 %add_convert_fusion = bf16[768,1536]{1,0:T(8,128)(2,1)} fusion(bf16[768,1536]{1,0:T(8,128)(2,1)} %bitcast.50, bf16[768,768]{1,0:T(8,128)(2,1)} %select_convert_fusion, bf16[768,1536]{1,0:T(8,128)(2,1)S(1)} %bitcast.45, bf16[1536,1536]{1,0:T(8,128)(2,1)} %fusion.8), kind=kOutput, calls=%fused_computation.13 | convolution fusion | flops 5440536576 | bytes 12976128 | tf_op jit(solution)/shard_map/dot_general | solution.py:288
  122.7 57.6 %all_to_all.21 = bf16[16,48,1536]{2,1,0:T(8,128)(2,1)S(1)} all-to-all(bf16[16,48,1536]{2,1,0:T(8,128)(2,1)} %get-tuple-element.218), channel_id=1, replica_groups=mesh['mem'=16,'tile'=16] {'tile'}, dimensions={0} | all-to-all | bytes 4718592 | tf_op jit(solution)/shard_map/all_to_all | solution.py:301
  180.5 2.6 %copy.16 = bf16[1,16,45,1440]{3,1,2,0:T(8,128)(2,1)} copy(bf16[1,16,45,1440]{3,2,1,0:T(8,128)(2,1)S(1)} %slice_bitcast_fusion) | data formatting | bytes 4147200 | tf_op jit(solution)/shard_map/broadcast_in_dim | solution.py:386
  (36 shorter events, 2.1 us)
Async XLA Ops:
  4.5 10.4 %copy-start.14 = (f32[16]{0:T(128)S(1)}, f32[16]{0:T(128)}, u32[]{:S(2)}) copy-start(f32[16]{0:T(128)} %param.17) | copy-start | bytes 196
  4.5 11.5 %copy-start.15 = (f32[16]{0:T(128)S(1)}, f32[16]{0:T(128)}, u32[]{:S(2)}) copy-start(f32[16]{0:T(128)} %param.16) | copy-start | bytes 196
  4.5 64.2 %all-to-all-start.1 = ((bf16[16,48,1536]{2,1,0:T(8,128)(2,1)}), bf16[16,48,1536]{2,1,0:T(8,128)(2,1)S(1)}, u32[]{:S(2)}, u32[]{:S(2)}) async-start(bf16[16,48,1536]{2,1,0:T(8,128)(2,1)} %pad.7), calls=%async_computation.1 | async-start | bytes 4718592 | tf_op jit(solution)/shard_map/all_to_all | solution.py:301
  20.6 9.2 %copy-start.1 = (bf16[16,48,1536]{2,1,0:T(8,128)(2,1)}, bf16[16,48,1536]{2,1,0:T(8,128)(2,1)S(1)}, u32[]{:S(2)}) copy-start(bf16[16,48,1536]{2,1,0:T(8,128)(2,1)S(1)} %pad.8.table_ref) | copy-start | bytes 7077892
  23.1 6.5 %copy-start.4 = (s32[1,16384]{1,0:T(1,128)S(1)}, s32[1,16384]{1,0:T(1,128)}, u32[]{:S(2)}) copy-start(s32[1,16384]{1,0:T(1,128)} %param.20) | copy-start | bytes 196612
  23.1 6.5 %copy-start.5 = (s32[1,16384]{1,0:T(1,128)S(1)}, s32[1,16384]{1,0:T(1,128)}, u32[]{:S(2)}) copy-start(s32[1,16384]{1,0:T(1,128)} %param.19) | copy-start | bytes 196612
  23.1 6.7 %copy-start.8 = (s32[1,16384]{1,0:T(1,128)S(1)}, s32[1,16384]{1,0:T(1,128)}, u32[]{:S(2)}) copy-start(s32[1,16384]{1,0:T(1,128)} %param.18) | copy-start | bytes 196612
  23.1 6.7 %copy-start.10 = (f32[1,16384]{1,0:T(1,128)S(1)}, f32[1,16384]{1,0:T(1,128)}, u32[]{:S(2)}) copy-start(f32[1,16384]{1,0:T(1,128)} %param.23) | copy-start | bytes 196612
  23.1 6.7 %copy-start.12 = (f32[1,16384]{1,0:T(1,128)S(1)}, f32[1,16384]{1,0:T(1,128)}, u32[]{:S(2)}) copy-start(f32[1,16384]{1,0:T(1,128)} %param.22) | copy-start | bytes 196612
  29.8 26.1 %copy-start.6 = (s32[1,16384]{1,0:T(1,128)}, s32[1,16384]{1,0:T(1,128)S(1)}, u32[]{:S(2)}) copy-start(s32[1,16384]{1,0:T(1,128)S(1)} %and_add_fusion) | copy-start | bytes 196612
  68.7 15.5 %copy-start = (bf16[16,48,1536]{2,1,0:T(8,128)(2,1)}, bf16[16,48,1536]{2,1,0:T(8,128)(2,1)S(1)}, u32[]{:S(2)}) copy-start(bf16[16,48,1536]{2,1,0:T(8,128)(2,1)S(1)} %all-to-all-done.1) | copy-start | bytes 7077892
  68.7 18.1 %all-to-all-start.2 = ((f32[16,40,128]{2,1,0:T(8,128)}), f32[16,40,128]{2,1,0:T(8,128)S(1)}, u32[]{:S(2)}, u32[]{:S(2)}) async-start(f32[16,40,128]{2,1,0:T(8,128)} %pack_slots.2), calls=%async_computation.2 | async-start | bytes 655360 | tf_op jit(solution)/shard_map/all_to_all | solution.py:301
  92.1 1.4 collective-permute-start.4
  93.5 4.4 %collective-permute-start.5 = (f32[144,128]{1,0:T(8,128)S(1)}, f32[144,128]{1,0:T(8,128)S(1)}, u32[]{:S(2)}, u32[]{:S(2)}) collective-permute-start(f32[144,128]{1,0:T(8,128)S(1)} %add.104), channel_id=1, source_target_pairs={{0,32},{16,48},{32,0},{48,16},{64,96},{80,112},{96,64},{112,80},{1... | collective-permute-start | bytes 221192 | tf_op jit(solution)/shard_map/ppermute | solution.py:295
  98.0 5.9 %collective-permute-start.6 = (f32[144,128]{1,0:T(8,128)S(1)}, f32[144,128]{1,0:T(8,128)S(1)}, u32[]{:S(2)}, u32[]{:S(2)}) collective-permute-start(f32[144,128]{1,0:T(8,128)S(1)} %add.105), channel_id=1, source_target_pairs={{0,64},{16,80},{32,96},{48,112},{64,0},{80,16},{96,32},{112,48},{1... | collective-permute-start | bytes 221192 | tf_op jit(solution)/shard_map/ppermute | solution.py:295
  103.9 5.9 %collective-permute-start.7 = (f32[144,128]{1,0:T(8,128)S(1)}, f32[144,128]{1,0:T(8,128)S(1)}, u32[]{:S(2)}, u32[]{:S(2)}) collective-permute-start(f32[144,128]{1,0:T(8,128)S(1)} %add.106), channel_id=1, source_target_pairs={{0,128},{16,144},{32,160},{48,176},{64,192},{80,208},{96,224},{112... | collective-permute-start | bytes 221192 | tf_op jit(solution)/shard_map/ppermute | solution.py:295

commit v5 on v4

--- a/solution.py
+++ b/solution.py
@@ -290,10 +290,9 @@
 
 def sum_members(value):
     members = lax.axis_size("mem")
-    step = 1
-    while step < members:
+    steps = [1 << bit for bit in range(members.bit_length() - 1)]
+    for step in steps[:1] + steps[:0:-1]:
         value = value + lax.ppermute(value, "mem", [(i, i ^ step) for i in range(members)])
-        step *= 2
     return value
 
 

time: 184 us -> 184 us (level)
  no operation moved by 1% of the time
where the time goes in v5:
time: 184 us; the launch traced here: 183 us
  blocking collectives  57.6 us (31%)
  Pallas kernels  34.9 us (19%)
  starting transfers between devices  24.1 us (13%)
  waiting for transfers between devices  24 us (13%)
  matrix products  18.2 us (10%)
  local copies, waits for them, and re-layouts  11.7 us (6%)
  other arithmetic  9.87 us (5%)
  between operations  2.78 us (2%)
    all_to_all x1, blocking collectives, exchange(): lax.all_to_all(value, 'tile', split_axis=0, concat_axis=0, tiled=True)  57.6 us
    pallas_call x1, Pallas kernels, pack_slots(): pl.pallas_call(pack_kernel, out_shape=jax.ShapeDtypeStruct((levels, SEND_...  26 us
    dot_general x2, matrix products, localize(): return jnp.dot(lat_root, zonal, preferred_element_type=F32)  18.2 us
    all_to_all x2, starting transfers between devices, exchange(): lax.all_to_all(value, 'tile', split_axis=0, concat_axis=0, tiled=True)  16.2 us
    all_to_all x2, waiting for transfers between devices, exchange(): lax.all_to_all(value, 'tile', split_axis=0, concat_axis=0, tiled=True)  15.5 us
    convert_element_type x2, other arithmetic, square_root(): return values.astype(BF16)  8.93 us
    ppermute x4, waiting for transfers between devices, sum_members(): lax.ppermute(value, 'mem', [(i, i ^ step) for i in range(members)])  8.51 us
    ppermute x4, starting transfers between devices, sum_members(): lax.ppermute(value, 'mem', [(i, i ^ step) for i in range(members)])  7.86 us
  transfers between devices with their start and end apart: 6, of which 6 were waited for; matrix products, arithmetic and copies ran while one was open for 13% of the time, Pallas kernels for 14%

profile of v5, /device:TPU:32, one launch (start us, length us, event | category | flops | bytes accessed | tf_op | source)
XLA Modules:
  0.0 183.1 jit_solution(16602877390831653786)
XLA Ops:
  0.0 2.8 %copy.20 = bf16[1,16,45,1440]{3,2,1,0:T(8,128)(2,1)S(1)} copy(bf16[1,16,45,1440]{3,1,2,0:T(8,128)(2,1)} %param.14) | data formatting | bytes 4147200 | tf_op args[0]
  2.8 1.7 pad.7
  4.5 9.6 %all-to-all-start.1 = ((bf16[16,48,1536]{2,1,0:T(8,128)(2,1)}), bf16[16,48,1536]{2,1,0:T(8,128)(2,1)S(1)}, u32[]{:S(2)}, u32[]{:S(2)}) async-start(bf16[16,48,1536]{2,1,0:T(8,128)(2,1)} %pad.7), calls=%async_computation.1 | async-start | bytes 4718592 | tf_op jit(solution)/shard_map/all_to_all | solution.py:300
  17.5 2.8 %copy.19 = bf16[1,16,45,1440]{3,2,1,0:T(8,128)(2,1)S(1)} copy(bf16[1,16,45,1440]{3,1,2,0:T(8,128)(2,1)} %param.15) | data formatting | bytes 4147200 | tf_op args[1]
  20.6 2.5 %select_convert_fusion = bf16[768,768]{1,0:T(8,128)(2,1)} fusion(f32[]{:T(128)S(6)} %sqrt.7, f32[]{:T(128)} %bitcast.15, f32[768]{0:T(1024)S(1)} %fusion.11, pred[768]{0:T(1024)(128)(4,1)S(1)} %fusion.15), kind=kLoop, calls=%fused_computation.20 | loop fusion | flops 5898240 | bytes 1183496 | tf_op jit(solution)/shard_map/convert_element_type | solution.py:37
  23.1 6.4 %fusion.8 = bf16[1536,1536]{1,0:T(8,128)(2,1)} fusion(f32[]{:T(128)S(6)} %sqrt.6, f32[]{:T(128)} %bitcast.14, f32[1536]{0:T(1024)S(1)} %iota_convert_fusion, pred[1536]{0:T(1024)(128)(4,1)S(1)} %iota_compare_fusion), kind=kLoop, calls=%fused_computation.12 | loop fusion | flops 28311552 | bytes 4726280 | tf_op jit(solution)/shard_map/convert_element_type | solution.py:37
  29.8 26.0 %pack_slots.2 = f32[16,40,128]{2,1,0:T(8,128)} custom-call(s32[2]{0:T(128)S(1)} %pad_add_fusion.1.scalar_ref, s32[128,128]{1,0:T(8,128)S(1)} %bitcast.56, s32[128,128]{1,0:T(8,128)S(1)} %bitcast.54, f32[128,128]{1,0:T(8,128)S(1)} %bitcast.58, f32[128,128]{1,0:T(8,128)S(1)} %bitcast.60, bf16[16,48,1536]{2,1,0:T(8,128)(2,1)S(1)} %pad.8.table_ref), custom_call_target="tpu_custom_call" | custom-call | flops 24999999488 | bytes 4194304 | tf_op jit(solution)/shard_map/pack_slots/pallas_call | solution.py:190
  55.8 12.9 %all-to-all-done.1 = bf16[16,48,1536]{2,1,0:T(8,128)(2,1)S(1)} async-done(((bf16[16,48,1536]{2,1,0:T(8,128)(2,1)}), bf16[16,48,1536]{2,1,0:T(8,128)(2,1)S(1)}, u32[]{:S(2)}, u32[]{:S(2)}) %all-to-all-start.1) | async-done | bytes 2359328 | tf_op jit(solution)/shard_map/all_to_all | solution.py:300
  68.7 6.6 %all-to-all-start.2 = ((f32[16,40,128]{2,1,0:T(8,128)}), f32[16,40,128]{2,1,0:T(8,128)S(1)}, u32[]{:S(2)}, u32[]{:S(2)}) async-start(f32[16,40,128]{2,1,0:T(8,128)} %pack_slots.2), calls=%async_computation.2 | async-start | bytes 655360 | tf_op jit(solution)/shard_map/all_to_all | solution.py:300
  75.3 8.9 %convolution_convert_fusion.2 = bf16[768,1536]{1,0:T(8,128)(2,1)} fusion(bf16[768,768]{1,0:T(8,128)(2,1)} %select_convert_fusion, bf16[768,1536]{1,0:T(8,128)(2,1)S(1)} %bitcast.49, bf16[1536,1536]{1,0:T(8,128)(2,1)} %fusion.8), kind=kOutput, calls=%fused_computation.15 | convolution fusion | flops 5438177280 | bytes 10616832 | tf_op jit(solution)/shard_map/dot_general | solution.py:288
  84.1 2.6 %all-to-all-done.2.run_ref = f32[16,40,128]{2,1,0:T(8,128)S(1)} async-done(((f32[16,40,128]{2,1,0:T(8,128)}), f32[16,40,128]{2,1,0:T(8,128)S(1)}, u32[]{:S(2)}, u32[]{:S(2)}) %all-to-all-start.2) | async-done | bytes 327712 | tf_op jit(solution)/shard_map/all_to_all | solution.py:300
  86.8 5.4 %slot_terms.2 = f32[144,128]{1,0:T(8,128)S(1)} custom-call(bf16[16,48,1536]{2,1,0:T(8,128)(2,1)} %bitcast.62, f32[16,40,128]{2,1,0:T(8,128)S(1)} %all-to-all-done.2.run_ref), custom_call_target="tpu_custom_call" | custom-call | flops 4000000000 | bytes 3145728 | tf_op jit(solution)/shard_map/slot_terms/pallas_call | solution.py:225
  92.2 1.3 collective-permute-done.4
  93.5 2.8 %collective-permute-start.5 = (f32[144,128]{1,0:T(8,128)S(1)}, f32[144,128]{1,0:T(8,128)S(1)}, u32[]{:S(2)}, u32[]{:S(2)}) collective-permute-start(f32[144,128]{1,0:T(8,128)S(1)} %add.104), channel_id=1, source_target_pairs={{0,128},{16,144},{32,160},{48,176},{64,192},{80,208},{96,224},{112... | collective-permute-start | bytes 221192 | tf_op jit(solution)/shard_map/ppermute | solution.py:295
  96.3 3.1 %collective-permute-done.5 = f32[144,128]{1,0:T(8,128)S(1)} collective-permute-done((f32[144,128]{1,0:T(8,128)S(1)}, f32[144,128]{1,0:T(8,128)S(1)}, u32[]{:S(2)}, u32[]{:S(2)}) %collective-permute-start.5) | collective-permute-done | bytes 73760 | tf_op jit(solution)/shard_map/ppermute | solution.py:295
  99.5 3.3 %collective-permute-start.6 = (f32[144,128]{1,0:T(8,128)S(1)}, f32[144,128]{1,0:T(8,128)S(1)}, u32[]{:S(2)}, u32[]{:S(2)}) collective-permute-start(f32[144,128]{1,0:T(8,128)S(1)} %add.105), channel_id=1, source_target_pairs={{0,64},{16,80},{32,96},{48,112},{64,0},{80,16},{96,32},{112,48},{1... | collective-permute-start | bytes 221192 | tf_op jit(solution)/shard_map/ppermute | solution.py:295
  102.8 2.7 %collective-permute-done.6 = f32[144,128]{1,0:T(8,128)S(1)} collective-permute-done((f32[144,128]{1,0:T(8,128)S(1)}, f32[144,128]{1,0:T(8,128)S(1)}, u32[]{:S(2)}, u32[]{:S(2)}) %collective-permute-start.6) | collective-permute-done | bytes 73760 | tf_op jit(solution)/shard_map/ppermute | solution.py:295
  105.4 1.7 collective-permute-start.7
  107.1 0.7 slice_reduce_fusion
  108.4 1.5 collective-permute-done.7
  109.9 3.5 %add_slots.2 = bf16[16,48,1536]{2,1,0:T(8,128)(2,1)S(1)} custom-call(f32[16,40,128]{2,1,0:T(8,128)S(1)} %all-to-all-done.2.run_ref, f32[144,128]{1,0:T(8,128)S(1)} %add.107.model_ref), custom_call_target="tpu_custom_call" | custom-call | flops 4000000000 | bytes 3145728 | tf_op jit(solution)/shard_map/add_slots/pallas_call | solution.py:275
  113.4 9.3 %add_convert_fusion = bf16[768,1536]{1,0:T(8,128)(2,1)} fusion(bf16[768,1536]{1,0:T(8,128)(2,1)} %bitcast.50, bf16[768,768]{1,0:T(8,128)(2,1)} %select_convert_fusion, bf16[768,1536]{1,0:T(8,128)(2,1)S(1)} %bitcast.45, bf16[1536,1536]{1,0:T(8,128)(2,1)} %fusion.8), kind=kOutput, calls=%fused_computation.13 | convolution fusion | flops 5440536576 | bytes 12976128 | tf_op jit(solution)/shard_map/dot_general | solution.py:288
  122.7 57.6 %all_to_all.21 = bf16[16,48,1536]{2,1,0:T(8,128)(2,1)S(1)} all-to-all(bf16[16,48,1536]{2,1,0:T(8,128)(2,1)} %get-tuple-element.218), channel_id=1, replica_groups=mesh['mem'=16,'tile'=16] {'tile'}, dimensions={0} | all-to-all | bytes 4718592 | tf_op jit(solution)/shard_map/all_to_all | solution.py:300
  180.5 2.6 %copy.16 = bf16[1,16,45,1440]{3,1,2,0:T(8,128)(2,1)} copy(bf16[1,16,45,1440]{3,2,1,0:T(8,128)(2,1)S(1)} %slice_bitcast_fusion) | data formatting | bytes 4147200 | tf_op jit(solution)/shard_map/broadcast_in_dim | solution.py:385
  (36 shorter events, 2.1 us)
Async XLA Ops:
  4.5 10.4 %copy-start.14 = (f32[16]{0:T(128)S(1)}, f32[16]{0:T(128)}, u32[]{:S(2)}) copy-start(f32[16]{0:T(128)} %param.17) | copy-start | bytes 196
  4.5 11.5 %copy-start.15 = (f32[16]{0:T(128)S(1)}, f32[16]{0:T(128)}, u32[]{:S(2)}) copy-start(f32[16]{0:T(128)} %param.16) | copy-start | bytes 196
  4.5 64.2 %all-to-all-start.1 = ((bf16[16,48,1536]{2,1,0:T(8,128)(2,1)}), bf16[16,48,1536]{2,1,0:T(8,128)(2,1)S(1)}, u32[]{:S(2)}, u32[]{:S(2)}) async-start(bf16[16,48,1536]{2,1,0:T(8,128)(2,1)} %pad.7), calls=%async_computation.1 | async-start | bytes 4718592 | tf_op jit(solution)/shard_map/all_to_all | solution.py:300
  20.6 9.2 %copy-start.1 = (bf16[16,48,1536]{2,1,0:T(8,128)(2,1)}, bf16[16,48,1536]{2,1,0:T(8,128)(2,1)S(1)}, u32[]{:S(2)}) copy-start(bf16[16,48,1536]{2,1,0:T(8,128)(2,1)S(1)} %pad.8.table_ref) | copy-start | bytes 7077892
  23.1 6.5 %copy-start.4 = (s32[1,16384]{1,0:T(1,128)S(1)}, s32[1,16384]{1,0:T(1,128)}, u32[]{:S(2)}) copy-start(s32[1,16384]{1,0:T(1,128)} %param.20) | copy-start | bytes 196612
  23.1 6.5 %copy-start.5 = (s32[1,16384]{1,0:T(1,128)S(1)}, s32[1,16384]{1,0:T(1,128)}, u32[]{:S(2)}) copy-start(s32[1,16384]{1,0:T(1,128)} %param.19) | copy-start | bytes 196612
  23.1 6.7 %copy-start.8 = (s32[1,16384]{1,0:T(1,128)S(1)}, s32[1,16384]{1,0:T(1,128)}, u32[]{:S(2)}) copy-start(s32[1,16384]{1,0:T(1,128)} %param.18) | copy-start | bytes 196612
  23.1 6.7 %copy-start.10 = (f32[1,16384]{1,0:T(1,128)S(1)}, f32[1,16384]{1,0:T(1,128)}, u32[]{:S(2)}) copy-start(f32[1,16384]{1,0:T(1,128)} %param.23) | copy-start | bytes 196612
  23.1 6.7 %copy-start.12 = (f32[1,16384]{1,0:T(1,128)S(1)}, f32[1,16384]{1,0:T(1,128)}, u32[]{:S(2)}) copy-start(f32[1,16384]{1,0:T(1,128)} %param.22) | copy-start | bytes 196612
  29.8 26.1 %copy-start.6 = (s32[1,16384]{1,0:T(1,128)}, s32[1,16384]{1,0:T(1,128)S(1)}, u32[]{:S(2)}) copy-start(s32[1,16384]{1,0:T(1,128)S(1)} %and_add_fusion) | copy-start | bytes 196612
  68.7 15.5 %copy-start = (bf16[16,48,1536]{2,1,0:T(8,128)(2,1)}, bf16[16,48,1536]{2,1,0:T(8,128)(2,1)S(1)}, u32[]{:S(2)}) copy-start(bf16[16,48,1536]{2,1,0:T(8,128)(2,1)S(1)} %all-to-all-done.1) | copy-start | bytes 7077892
  68.7 18.1 %all-to-all-start.2 = ((f32[16,40,128]{2,1,0:T(8,128)}), f32[16,40,128]{2,1,0:T(8,128)S(1)}, u32[]{:S(2)}, u32[]{:S(2)}) async-start(f32[16,40,128]{2,1,0:T(8,128)} %pack_slots.2), calls=%async_computation.2 | async-start | bytes 655360 | tf_op jit(solution)/shard_map/all_to_all | solution.py:300
  92.1 1.4 collective-permute-start.4
  93.5 5.9 %collective-permute-start.5 = (f32[144,128]{1,0:T(8,128)S(1)}, f32[144,128]{1,0:T(8,128)S(1)}, u32[]{:S(2)}, u32[]{:S(2)}) collective-permute-start(f32[144,128]{1,0:T(8,128)S(1)} %add.104), channel_id=1, source_target_pairs={{0,128},{16,144},{32,160},{48,176},{64,192},{80,208},{96,224},{112... | collective-permute-start | bytes 221192 | tf_op jit(solution)/shard_map/ppermute | solution.py:295
  99.5 5.9 %collective-permute-start.6 = (f32[144,128]{1,0:T(8,128)S(1)}, f32[144,128]{1,0:T(8,128)S(1)}, u32[]{:S(2)}, u32[]{:S(2)}) collective-permute-start(f32[144,128]{1,0:T(8,128)S(1)} %add.105), channel_id=1, source_target_pairs={{0,64},{16,80},{32,96},{48,112},{64,0},{80,16},{96,32},{112,48},{1... | collective-permute-start | bytes 221192 | tf_op jit(solution)/shard_map/ppermute | solution.py:295
  105.4 4.4 %collective-permute-start.7 = (f32[144,128]{1,0:T(8,128)S(1)}, f32[144,128]{1,0:T(8,128)S(1)}, u32[]{:S(2)}, u32[]{:S(2)}) collective-permute-start(f32[144,128]{1,0:T(8,128)S(1)} %add.106), channel_id=1, source_target_pairs={{0,32},{16,48},{32,0},{48,16},{64,96},{80,112},{96,64},{112,80},{1... | collective-permute-start | bytes 221192 | tf_op jit(solution)/shard_map/ppermute | solution.py:295
